TPU v7x, 32 devices: a whole 2x2x4 slice. The times are simulated.
32 devices in a mesh: seq: 8 (over z, x), tp: 4 (over y, core).
Axes of the slice: x: 2, y: 2, z: 4, core: 2. Of those that a mesh axis runs over, the one named last changes fastest.
Arguments:
- tokens: bfloat16 [4096, 4096], P(('seq', 'tp')), may hold values from -64 to 64, as said below
- joined_projection_weight: bfloat16 [4096, 6144], P(None, 'tp'), may hold values from -0.09375 to 0.09375
- adapter_down_weight: bfloat16 [4096, 64], replicated, may hold values from -0.09375 to 0.09375
- adapter_up_weight: bfloat16 [64, 6144], P(None, 'tp'), may hold values from -0.75 to 0.75
- document_index: int32 [4096], replicated, may hold values from 0 to 3, as said below
- query_to_key_head: int32 [32], replicated, may hold values from 0 to 7, as said below
Outputs:
- context: bfloat16 [4096, 4096], P(('seq', 'tp'))
Inputs may be any that keep to these rules, and one draw needn't show every extreme that they name: `tokens`: rows of order one, except in the hidden draw where some rows have larger scales. `query_to_key_head`: each of 0 to 7 is named by exactly 4 query heads. `document_index`: never falling, starting at 0; each of the 4 documents covers 4096 / 16 or more positions.
All inputs are finite; a program needn't handle non-finite values.
Results may differ from a plain program's by a relative error of at most 0.012.
The roundings to bfloat16 on the way count: a program that leaves them out, or rounds other values in their place, can miss the bound.
Values may be sent and summed in bfloat16 or wider, within the bound.
A program may use at most 128 MiB of HBM per device.

v0:
```python
import functools

import jax
import jax.numpy as jnp
from jax import lax
from jax.experimental import pallas as pl
from jax.experimental.pallas import tpu as pltpu
from jax.sharding import PartitionSpec as P

H = 32
KV = 8
DH = 128
GROUP = H // KV

ADAPTER_SCALE = 0.5
THETA = 500000.0
NEG_BIG = -1e30
LOG2_E = 1.4426950408889634


def rope_tables(places):
    half = DH // 2
    frequency = THETA ** (-(jnp.arange(half, dtype=jnp.float32) * 2.0) / DH)
    angles = places[:, None] * frequency[None, :]
    cosine, sine = jnp.cos(angles), jnp.sin(angles)
    return jnp.concatenate([cosine, cosine], 1), jnp.concatenate([-sine, sine], 1)


MESH = pl.DeviceIdType.MESH


def front_kernel(
    rotated_pairs, here, index_ref, tokens_ref, w_ref, down_ref, up_ref, cos_ref, sin_ref,
    q_ref, kv_ref,
    x_all, w_all, stage, landed_low, landed_high, sent, mid_ref,
    w_sem, local_sem, send_sem, x_sem, land_sem, q_sem, kv_sem, spread_sem,
):
    tp = lax.axis_index("tp")
    seq = lax.axis_index("seq")
    chips, _, own, _ = x_all.shape
    halves, half = 2, own // 2
    tp_count, seq_count = 2 * chips, q_ref.shape[0]
    steps = w_all.shape[0]
    wide = w_all.shape[2]
    pair = wide // DH
    chip, core = tp // 2, tp % 2
    partner = chip * 2 + (1 - core)
    landed = (landed_low, landed_high)
    sends = []

    def send(src, dst, sem, axis, target):
        copy = pltpu.make_async_remote_copy(
            src_ref=src, dst_ref=dst, send_sem=send_sem.at[len(sends)], recv_sem=sem,
            device_id={axis: target}, device_id_type=MESH,
        )
        copy.start()
        sends.append(copy)

    def arrived(dst, sem, axis, source):
        pltpu.make_async_remote_copy(
            src_ref=dst, dst_ref=dst, send_sem=send_sem.at[0], recv_sem=sem,
            device_id={axis: source}, device_id_type=MESH,
        ).wait_recv()

    def weight_copy(step):
        return pltpu.make_async_copy(
            w_ref.at[:, pl.ds(pl.multiple_of(step * wide, wide), wide)], w_all.at[step], w_sem.at[step]
        )

    own_copy = pltpu.make_async_copy(tokens_ref, x_all.at[chip, core], local_sem.at[0])
    own_copy.start()
    for step in range(steps):
        weight_copy(step).start()

    barrier = pltpu.get_barrier_semaphore()
    for k in range(1, tp_count):
        pl.semaphore_signal(
            barrier, inc=1, device_id={"tp": (tp + k) % tp_count}, device_id_type=MESH
        )
    for k in range(1, seq_count):
        pl.semaphore_signal(
            barrier, inc=1, device_id={"seq": (seq + k) % seq_count}, device_id_type=MESH
        )
    pl.semaphore_wait(barrier, tp_count - 1 + seq_count - 1)

    def rows_of(h):
        return pl.ds(h * half, half)

    others = [(chip + k) % chips for k in range(1, chips)]
    for h in range(halves):
        for other in others:
            send(
                tokens_ref.at[rows_of(h)], x_all.at[chip, core, rows_of(h)],
                x_sem.at[chip, core, h], "tp", other * 2 + core,
            )
        send(
            tokens_ref.at[rows_of(h)], x_all.at[chip, core, rows_of(h)],
            x_sem.at[chip, core, h], "tp", partner,
        )

    def compute(where, low, count, first):
        rows = pl.ds(low, count)
        x = x_all[where, :, rows, :].reshape(2 * count, x_all.shape[3])
        mid_ref[pl.ds(0, 2 * count)] = lax.dot_general(
            x, down_ref[...], (((1,), (1,)), ((), ())), preferred_element_type=jnp.float32
        ).astype(jnp.bfloat16)

        @pl.loop(0, steps)
        def _(step):
            if first:
                weight_copy(step).wait()
            x = x_all[where, :, rows, :].reshape(2 * count, x_all.shape[3])
            joined = jnp.dot(x, w_all[step], preferred_element_type=jnp.float32)
            joined = joined + ADAPTER_SCALE * jnp.dot(
                mid_ref[pl.ds(0, 2 * count)], up_ref[:, pl.ds(pl.multiple_of(step * wide, wide), wide)],
                preferred_element_type=jnp.float32
            )
            kind = step // rotated_pairs
            cosine = cos_ref[kind, where, :, rows, :].reshape(2 * count, DH)
            sine = sin_ref[kind, where, :, rows, :].reshape(2 * count, DH)
            for head in range(pair):
                part = joined[:, head * DH : (head + 1) * DH]
                part = part * cosine + pltpu.roll(part, DH // 2, 1) * sine
                part = part.astype(jnp.bfloat16)
                for k in range(2):
                    stage[where, k, step * pair + head, rows] = part[k * count : (k + 1) * count]

    def give(where, k, h, target):
        send(
            stage.at[where, k, :, rows_of(h)], landed[h].at[tp],
            land_sem.at[tp, h], "tp", target,
        )

    own_copy.wait()
    for h in range(halves):
        arrived(x_all.at[chip, 1 - core, rows_of(h)], x_sem.at[chip, 1 - core, h], "tp", partner)
    compute(chip, 0, own, True)
    keeps = [
        pltpu.make_async_copy(
            stage.at[chip, core, :, rows_of(h)], landed[h].at[tp], local_sem.at[5 * h]
        )
        for h in range(halves)
    ]
    for keep in keeps:
        keep.start()
    for h in range(halves):
        give(chip, 1 - core, h, partner)
    for h in range(halves):
        for other in others:
            block = x_all.at[other, core, rows_of(h)]
            arrived(block, x_sem.at[other, core, h], "tp", other * 2 + core)
            send(block, block, x_sem.at[other, core, h], "tp", partner)
        for other in others:
            arrived(
                x_all.at[other, 1 - core, rows_of(h)], x_sem.at[other, 1 - core, h], "tp", partner
            )
            compute(other, h * half, half, False)
            for k in range(2):
                give(other, k, h, other * 2 + k)
    for keep in keeps:
        keep.wait()
    q_per = H // tp_count
    kv_per = KV // tp_count
    near = [(seq + k) % seq_count for k in range(1, seq_count)]
    mine = []

    def hold(src, dst):
        copy = pltpu.make_async_copy(src, dst, local_sem.at[1 + len(mine)])
        copy.start()
        mine.append(copy)

    for h in range(halves):
        rows = rows_of(h)
        for k in range(1, tp_count):
            source = (tp + k) % tp_count
            arrived(landed[h].at[source], land_sem.at[source, h], "tp", source)

        @pl.loop(0, seq_count)
        def _(j):
            kv_head = j * here // GROUP
            for k in range(2):
                sent[j, here + k, rows] = landed[h][
                    kv_head // kv_per, q_per + k * kv_per + kv_head % kv_per
                ]

        for j in near:
            send(
                sent.at[j, pl.ds(here, 2), rows], kv_ref.at[tp, seq, :, rows],
                kv_sem.at[seq, h], "seq", j,
            )

        @pl.loop(0, seq_count)
        def _(j):
            for k in range(here):
                head = index_ref[j * here + k]
                sent[j, k, rows] = landed[h][head // q_per, head % q_per]

        for j in near:
            send(
                sent.at[j, pl.ds(0, here), rows], q_ref.at[seq, :, rows],
                q_sem.at[seq, h], "seq", j,
            )
        hold(sent.at[seq, pl.ds(here, 2), rows], kv_ref.at[tp, seq, :, rows])
        hold(sent.at[seq, pl.ds(0, here), rows], q_ref.at[seq, :, rows])

    for copy in mine:
        copy.wait()
    for h in range(halves):
        for n, source in enumerate([seq] + near[::-1]):
            block = kv_ref.at[tp, source, :, rows_of(h)]
            if n:
                arrived(block, kv_sem.at[source, h], "seq", source)
            for k in range(1, tp_count):
                send(block, block, spread_sem.at[tp, source, h], "tp", (tp + k) % tp_count)
    for h in range(halves):
        for source in near:
            arrived(q_ref.at[source, :, rows_of(h)], q_sem.at[source, h], "seq", source)
        for k in range(1, tp_count):
            source = (tp + k) % tp_count
            for n in range(seq_count):
                arrived(
                    kv_ref.at[source, n, :, rows_of(h)], spread_sem.at[source, n, h], "tp", source
                )
    for copy in sends:
        copy.wait_send()


def front(index, tokens, w, down, up, cosine, sine, tp_count, seq_count, rotated_heads):
    own, width = tokens.shape
    heads = w.shape[1] // DH
    pair = 2
    steps = heads // pair
    chips = tp_count // 2
    here = H // seq_count
    rank = down.shape[1]
    vmem = pl.BlockSpec(memory_space=pltpu.VMEM)
    anywhere = pl.BlockSpec(memory_space=pl.ANY)
    count = (
        2 * chips + 2 + 2 * (chips - 1) * 4 + 4 * (seq_count - 1) + 2 * seq_count * (tp_count - 1)
    )
    bf16 = jnp.bfloat16
    return pl.pallas_call(
        functools.partial(front_kernel, rotated_heads // pair, here),
        in_specs=[pl.BlockSpec(memory_space=pltpu.SMEM), anywhere, anywhere, vmem, vmem, vmem, vmem],
        out_specs=[anywhere, anywhere],
        out_shape=[
            jax.ShapeDtypeStruct((seq_count, here, own, DH), bf16),
            jax.ShapeDtypeStruct((tp_count, seq_count, 2, own, DH), bf16),
        ],
        scratch_shapes=[
            pltpu.VMEM((chips, 2, own, width), bf16),
            pltpu.VMEM((steps, width, pair * DH), bf16),
            pltpu.VMEM((chips, 2, heads, own, DH), bf16),
            pltpu.VMEM((tp_count, heads, own // 2, DH), bf16),
            pltpu.VMEM((tp_count, heads, own // 2, DH), bf16),
            pltpu.VMEM((seq_count, here + 2, own, DH), bf16),
            pltpu.VMEM((2 * own, rank), bf16),
            pltpu.SemaphoreType.DMA((steps,)),
            pltpu.SemaphoreType.DMA((6,)),
            pltpu.SemaphoreType.DMA((count,)),
            pltpu.SemaphoreType.DMA((chips, 2, 2)),
            pltpu.SemaphoreType.DMA((tp_count, 2)),
            pltpu.SemaphoreType.DMA((seq_count, 2)),
            pltpu.SemaphoreType.DMA((seq_count, 2)),
            pltpu.SemaphoreType.DMA((tp_count, seq_count, 2)),
        ],
        compiler_params=pltpu.CompilerParams(collective_id=0, has_side_effects=True),
        name="front",
    )(index, tokens, w, down.T, up, cosine, sine)


def finish_kernel(slot_ref, in_ref, out_ref, landed, send_sem, land_sem, local_sem):
    seq = lax.axis_index("seq")
    seq_count, here, _, _ = landed.shape
    own_copy = pltpu.make_async_copy(in_ref.at[seq], landed.at[seq], local_sem.at[0])
    own_copy.start()
    near = [(seq + k) % seq_count for k in range(1, seq_count)]
    barrier = pltpu.get_barrier_semaphore()
    for j in near:
        pl.semaphore_signal(barrier, inc=1, device_id={"seq": j}, device_id_type=MESH)
    pl.semaphore_wait(barrier, seq_count - 1)
    sends = []
    for n, j in enumerate(near):
        copy = pltpu.make_async_remote_copy(
            src_ref=in_ref.at[j], dst_ref=landed.at[seq], send_sem=send_sem.at[n],
            recv_sem=land_sem.at[seq], device_id={"seq": j}, device_id_type=MESH,
        )
        copy.start()
        sends.append(copy)
    own_copy.wait()
    for j in near:
        pltpu.make_async_remote_copy(
            src_ref=landed.at[j], dst_ref=landed.at[j], send_sem=send_sem.at[0],
            recv_sem=land_sem.at[j], device_id={"seq": j}, device_id_type=MESH,
        ).wait_recv()
    for head in range(seq_count * here):
        slot = slot_ref[head]
        out_ref[:, head * DH : (head + 1) * DH] = landed[slot // here, slot % here]
    for copy in sends:
        copy.wait_send()


def finish(slot, context):
    seq_count, here, rows, _ = context.shape
    return pl.pallas_call(
        finish_kernel,
        in_specs=[pl.BlockSpec(memory_space=pltpu.SMEM), pl.BlockSpec(memory_space=pl.ANY)],
        out_specs=pl.BlockSpec(memory_space=pltpu.VMEM),
        out_shape=jax.ShapeDtypeStruct((rows, seq_count * here * DH), context.dtype),
        scratch_shapes=[
            pltpu.VMEM(context.shape, context.dtype),
            pltpu.SemaphoreType.DMA((seq_count,)),
            pltpu.SemaphoreType.DMA((seq_count,)),
            pltpu.SemaphoreType.DMA((1,)),
        ],
        compiler_params=pltpu.CompilerParams(collective_id=1, has_side_effects=True),
        name="finish",
    )(slot, context)


def attend_kernel(heads, scalar_ref, q_ref, kv_ref, doc_ref, out_ref):
    step = pl.program_id(0)
    tp = lax.axis_index("tp")
    chunks, _, _, own, _ = kv_ref.shape
    block = chunks * own
    rows = heads * own
    q = q_ref[0, :heads].reshape(rows, DH)
    place = step * block + tp * own
    first = jnp.sum((doc_ref[...] < scalar_ref[place]).astype(jnp.int32))
    docs = doc_ref[pl.ds(step * chunks + tp, 1), :]
    docs = jnp.broadcast_to(docs, (own, own)).T[:, :1]
    docs = jnp.concatenate([docs] * heads, 0)
    places = place + lax.broadcasted_iota(jnp.int32, (own, 1), 0)
    places = jnp.concatenate([places] * heads, 0)
    factor = (DH**-0.5) * LOG2_E

    def body(index, carry, own_block=False):
        top, total, acc = carry
        keys = kv_ref[:, index, 0].reshape(block, DH)
        values = kv_ref[:, index, 1].reshape(block, DH)
        scores = lax.dot_general(
            q, keys, (((1,), (1,)), ((), ())), preferred_element_type=jnp.float32
        )
        at = index * block + lax.broadcasted_iota(jnp.int32, (1, block), 1)
        key_docs = jnp.concatenate(
            [doc_ref[pl.ds(index * chunks + c, 1), :] for c in range(chunks)], 1
        )
        kept = key_docs == docs
        if own_block:
            kept = kept & (at <= places)
        scores = jnp.where(kept, scores, NEG_BIG)
        new_top = jnp.maximum(top, jnp.max(scores, 1, keepdims=True))
        shrink = jnp.exp2((top - new_top) * factor)
        powers = jnp.exp2((scores - new_top) * factor)
        total = total * shrink + jnp.sum(powers, 1, keepdims=True)
        acc = acc * shrink + jnp.dot(
            powers.astype(jnp.bfloat16), values, preferred_element_type=jnp.float32
        )
        return new_top, total, acc

    last = place // block
    start = (
        jnp.full((rows, 1), NEG_BIG, jnp.float32),
        jnp.zeros((rows, 1), jnp.float32),
        jnp.zeros((rows, DH), jnp.float32),
    )
    carry = body(last, start, True)
    top, total, acc = lax.fori_loop(first // block, last, body, carry)
    out_ref[0] = (acc / total).astype(jnp.bfloat16).reshape(heads, own, DH)


def attend(document_index, q, kv, heads):
    steps, slabs, own, _ = q.shape
    return pl.pallas_call(
        functools.partial(attend_kernel, heads),
        grid_spec=pltpu.PrefetchScalarGridSpec(
            num_scalar_prefetch=1,
            grid=(steps,),
            in_specs=[
                pl.BlockSpec((1, slabs, own, DH), lambda i, *_: (i, 0, 0, 0)),
                pl.BlockSpec(kv.shape, lambda i, *_: (0,) * 5),
                pl.BlockSpec((steps * kv.shape[0], own), lambda i, *_: (0, 0)),
            ],
            out_specs=pl.BlockSpec((1, heads, own, DH), lambda i, *_: (i, 0, 0, 0)),
        ),
        out_shape=jax.ShapeDtypeStruct((steps, heads, own, DH), jnp.bfloat16),
        name="attend",
    )(document_index, q, kv, document_index.reshape(-1, own))


def head_tables(query_to_key_head):
    heads = jnp.arange(H, dtype=jnp.int32)
    same = query_to_key_head[:, None] == query_to_key_head[None, :]
    earlier = heads[None, :] < heads[:, None]
    slot = GROUP * query_to_key_head + jnp.sum((same & earlier).astype(jnp.int32), 1)
    order = jnp.sum(jnp.where(slot[None, :] == heads[:, None], heads[None, :], 0), 1)
    return order.astype(jnp.int32), slot.astype(jnp.int32)


def per_device(
    tokens,
    joined_projection_weight,
    adapter_down_weight,
    adapter_up_weight,
    document_index,
    query_to_key_head,
):
    tp_count = lax.axis_size("tp")
    seq_count = lax.axis_size("seq")
    tp_rank = lax.axis_index("tp")
    seq_rank = lax.axis_index("seq")
    own = tokens.shape[0]
    block = own * tp_count
    here = H // seq_count
    q_per, kv_per = H // tp_count, KV // tp_count

    index, slot = head_tables(query_to_key_head)
    places = (seq_rank * block + jnp.arange(block, dtype=jnp.int32)).astype(jnp.float32)
    cosine, sine = rope_tables(places)
    table = (1, tp_count // 2, 2, own, DH)
    cosine = jnp.concatenate([cosine.reshape(table), jnp.ones(table, jnp.float32)])
    sine = jnp.concatenate([sine.reshape(table), jnp.zeros(table, jnp.float32)])
    held, kv = front(
        index, tokens, joined_projection_weight, adapter_down_weight, adapter_up_weight,
        cosine, sine, tp_count, seq_count, q_per + kv_per,
    )
    context = attend(document_index, held, kv, here)
    return finish(slot, context)


def solution(mesh):
    return jax.shard_map(
        per_device,
        mesh=mesh,
        in_specs=(P(("seq", "tp"), None), P(None, "tp"), P(), P(None, "tp"), P(), P()),
        out_specs=P(("seq", "tp"), None),
        check_vma=False,
    )
```

profile of v0, /device:TPU:13, one launch (start us, length us, event | category | flops | bytes accessed | tf_op | source)
XLA Modules:
  0.0 124.4 jit_solution(1460311523905552101)
XLA Ops:
  0.0 0.9 convert_reduce_fusion
  0.9 0.7 multiply_add_fusion.slot_ref
  1.6 0.0 copy-start
  1.6 0.7 select_reduce_fusion.index_ref
  2.3 1.0 fusion
  3.3 1.2 select_maximum_fusion
  4.5 72.5 %front.1 = (bf16[8,4,128,128]{3,2,1,0:T(8,128)(2,1)}, bf16[4,8,2,128,128]{4,3,2,1,0:T(8,128)(2,1)}) custom-call(s32[32]{0:T(128)} %select_reduce_fusion.index_ref, bf16[128,4096]{1,0:T(8,128)(2,1)} %tokens_ref.1, bf16[4096,1536]{1,0:T(8,128)(2,1)} %w_ref.1, bf16[64,4096]{1,0:T(8,128)(2,1)} %bitcast.2, bf16[64,1536]{1,0:T(8,128)(2,1)} %up_ref.1, ...), custom_call_target="tpu_custom_call" | custom-call | tf_op jit(solution)/shard_map/front/pallas_call | solution.py:242
  77.0 17.2 %attend.1.in_ref = bf16[8,4,128,128]{3,2,1,0:T(8,128)(2,1)} custom-call(s32[4096]{0:T(1024)} %scalar_ref.1, bf16[8,4,128,128]{3,2,1,0:T(8,128)(2,1)} %get-tuple-element.7.q_ref, bf16[4,8,2,128,128]{4,3,2,1,0:T(8,128)(2,1)} %get-tuple-element.8.kv_ref, s32[32,128]{1,0:T(8,128)} %bitcast.3), custom_call_target="tpu_custom_call" | custom-call | tf_op jit(solution)/shard_map/attend/pallas_call | solution.py:374
  94.2 0.0 copy-done
  94.2 27.8 %finish.1 = bf16[128,4096]{1,0:T(8,128)(2,1)} custom-call(s32[32]{0:T(128)} %copy-done, bf16[8,4,128,128]{3,2,1,0:T(8,128)(2,1)} %attend.1.in_ref), custom_call_target="tpu_custom_call" | custom-call | tf_op jit(solution)/shard_map/finish/pallas_call | solution.py:305
  122.1 2.3 %copy.8 = bf16[128,4096]{1,0:T(8,128)(2,1)} copy(bf16[128,4096]{1,0:T(8,128)(2,1)} %finish.1) | data formatting | bytes 2097152
  (2 shorter events, 0.0 us)
Async XLA Ops:
  1.6 92.7 %copy-start = (s32[32]{0:T(128)}, s32[32]{0:T(128)S(1)}, u32[]{:S(2)}) copy-start(s32[32]{0:T(128)S(1)} %multiply_add_fusion.slot_ref) | copy-start | bytes 388
where the time goes:
time: 126 us; the launch traced here: 124 us
  Pallas kernels  118 us (94%)
  other arithmetic  4.47 us (4%)
  local copies, waits for them, and re-layouts  2.29 us (2%)
    pallas_call x1, Pallas kernels, front(): pl.pallas_call(functools.partial(front_kernel, rotated_heads // pair, her...  72.5 us
    pallas_call x1, Pallas kernels, finish(): pl.pallas_call(finish_kernel, in_specs=[pl.BlockSpec(memory_space=pltpu.S...  27.8 us
    pallas_call x1, Pallas kernels, attend(): pl.pallas_call(functools.partial(attend_kernel, heads), grid_spec=pltpu.P...  17.2 us

commit v1 on v0

--- a/solution.py
+++ b/solution.py
@@ -210,16 +210,24 @@
             block = kv_ref.at[tp, source, :, rows_of(h)]
             if n:
                 arrived(block, kv_sem.at[source, h], "seq", source)
-            for k in range(1, tp_count):
-                send(block, block, spread_sem.at[tp, source, h], "tp", (tp + k) % tp_count)
+            for other in others:
+                send(block, block, spread_sem.at[tp, source, h], "tp", other * 2 + core)
+            send(block, block, spread_sem.at[tp, source, h], "tp", partner)
+    for h in range(halves):
+        for source in [seq] + near[::-1]:
+            for other in others:
+                far = other * 2 + core
+                block = kv_ref.at[far, source, :, rows_of(h)]
+                arrived(block, spread_sem.at[far, source, h], "tp", far)
+                send(block, block, spread_sem.at[far, source, h], "tp", partner)
     for h in range(halves):
         for source in near:
             arrived(q_ref.at[source, :, rows_of(h)], q_sem.at[source, h], "seq", source)
-        for k in range(1, tp_count):
-            source = (tp + k) % tp_count
+        for k in range(chips):
+            source = (chip + k) % chips * 2 + 1 - core
             for n in range(seq_count):
                 arrived(
-                    kv_ref.at[source, n, :, rows_of(h)], spread_sem.at[source, n, h], "tp", source
+                    kv_ref.at[source, n, :, rows_of(h)], spread_sem.at[source, n, h], "tp", partner
                 )
     for copy in sends:
         copy.wait_send()

time: 126 us -> 126 us (level)
  the two profiles are of different devices: /device:TPU:13 before, /device:TPU:11 now
where the time goes in v1:
time: 126 us; the launch traced here: 125 us
  Pallas kernels  119 us (94%)
  other arithmetic  4.47 us (4%)
  local copies, waits for them, and re-layouts  2.29 us (2%)
    pallas_call x1, Pallas kernels, front(): pl.pallas_call(functools.partial(front_kernel, rotated_heads // pair, her...  73.2 us
    pallas_call x1, Pallas kernels, finish(): pl.pallas_call(finish_kernel, in_specs=[pl.BlockSpec(memory_space=pltpu.S...  29.3 us
    pallas_call x1, Pallas kernels, attend(): pl.pallas_call(functools.partial(attend_kernel, heads), grid_spec=pltpu.P...  16.2 us

profile of v1, /device:TPU:11, one launch (start us, length us, event | category | flops | bytes accessed | tf_op | source)
XLA Modules:
  0.0 125.4 jit_solution(15203032237248887358)
XLA Ops:
  0.0 0.9 convert_reduce_fusion
  0.9 0.7 multiply_add_fusion.slot_ref
  1.6 0.0 copy-start
  1.6 0.7 select_reduce_fusion.index_ref
  2.3 1.0 fusion
  3.3 1.2 select_maximum_fusion
  4.5 73.2 %front.1 = (bf16[8,4,128,128]{3,2,1,0:T(8,128)(2,1)}, bf16[4,8,2,128,128]{4,3,2,1,0:T(8,128)(2,1)}) custom-call(s32[32]{0:T(128)} %select_reduce_fusion.index_ref, bf16[128,4096]{1,0:T(8,128)(2,1)} %tokens_ref.1, bf16[4096,1536]{1,0:T(8,128)(2,1)} %w_ref.1, bf16[64,4096]{1,0:T(8,128)(2,1)} %bitcast.2, bf16[64,1536]{1,0:T(8,128)(2,1)} %up_ref.1, ...), custom_call_target="tpu_custom_call" | custom-call | tf_op jit(solution)/shard_map/front/pallas_call | solution.py:250
  77.7 16.2 %attend.1.in_ref = bf16[8,4,128,128]{3,2,1,0:T(8,128)(2,1)} custom-call(s32[4096]{0:T(1024)} %scalar_ref.1, bf16[8,4,128,128]{3,2,1,0:T(8,128)(2,1)} %get-tuple-element.7.q_ref, bf16[4,8,2,128,128]{4,3,2,1,0:T(8,128)(2,1)} %get-tuple-element.8.kv_ref, s32[32,128]{1,0:T(8,128)} %bitcast.3), custom_call_target="tpu_custom_call" | custom-call | tf_op jit(solution)/shard_map/attend/pallas_call | solution.py:382
  93.8 0.0 copy-done
  93.8 29.3 %finish.1 = bf16[128,4096]{1,0:T(8,128)(2,1)} custom-call(s32[32]{0:T(128)} %copy-done, bf16[8,4,128,128]{3,2,1,0:T(8,128)(2,1)} %attend.1.in_ref), custom_call_target="tpu_custom_call" | custom-call | tf_op jit(solution)/shard_map/finish/pallas_call | solution.py:313
  123.1 2.3 %copy.8 = bf16[128,4096]{1,0:T(8,128)(2,1)} copy(bf16[128,4096]{1,0:T(8,128)(2,1)} %finish.1) | data formatting | bytes 2097152
  (2 shorter events, 0.0 us)
Async XLA Ops:
  1.6 92.3 %copy-start = (s32[32]{0:T(128)}, s32[32]{0:T(128)S(1)}, u32[]{:S(2)}) copy-start(s32[32]{0:T(128)S(1)} %multiply_add_fusion.slot_ref) | copy-start | bytes 388

commit v2 on v0

v2 whole, which is shorter than its diff:
```python
import functools

import jax
import jax.numpy as jnp
from jax import lax
from jax.experimental import pallas as pl
from jax.experimental.pallas import tpu as pltpu
from jax.sharding import PartitionSpec as P

H = 32
KV = 8
DH = 128
GROUP = H // KV

ADAPTER_SCALE = 0.5
THETA = 500000.0
NEG_BIG = -1e30
LOG2_E = 1.4426950408889634


def rope_tables(places):
    half = DH // 2
    frequency = THETA ** (-(jnp.arange(half, dtype=jnp.float32) * 2.0) / DH)
    angles = places[:, None] * frequency[None, :]
    cosine, sine = jnp.cos(angles), jnp.sin(angles)
    return jnp.concatenate([cosine, cosine], 1), jnp.concatenate([-sine, sine], 1)


MESH = pl.DeviceIdType.MESH


def front_kernel(
    rotated_pairs, here, ahead, index_ref, tokens_ref, w_ref, down_ref, up_ref, cos_ref, sin_ref,
    q_ref, kv_ref,
    x_all, w_all, stage, sent, mid_ref,
    w_sem, own_sem, keep_sem, hold_sem, send_sem, x_sem, land_sem, q_sem, kv_sem, spread_sem,
    *landed,
):
    tp = lax.axis_index("tp")
    seq = lax.axis_index("seq")
    chips, _, own, width = x_all.shape
    parts, part = len(landed), landed[0].shape[2]
    tp_count, seq_count = 2 * chips, q_ref.shape[0]
    steps = w_all.shape[0]
    wide = w_all.shape[2]
    pair = wide // DH
    chip, core = tp // 2, tp % 2
    partner = chip * 2 + (1 - core)
    others = [(chip + k) % chips for k in range(1, chips)]
    near = [(seq + k) % seq_count for k in range(1, seq_count)]
    q_per = H // tp_count
    kv_per = KV // tp_count
    sends = []
    locals_ = []

    def send(src, dst, sem, axis, target):
        copy = pltpu.make_async_remote_copy(
            src_ref=src, dst_ref=dst, send_sem=send_sem.at[len(sends)], recv_sem=sem,
            device_id={axis: target}, device_id_type=MESH,
        )
        copy.start()
        sends.append(copy)

    def arrived(dst, sem, axis, source):
        pltpu.make_async_remote_copy(
            src_ref=dst, dst_ref=dst, send_sem=send_sem.at[0], recv_sem=sem,
            device_id={axis: source}, device_id_type=MESH,
        ).wait_recv()

    def weight_copy(step):
        return pltpu.make_async_copy(
            w_ref.at[:, pl.ds(pl.multiple_of(step * wide, wide), wide)], w_all.at[step], w_sem.at[step]
        )

    def rows_of(c):
        return pl.ds(c * part, part)

    own_copy = pltpu.make_async_copy(tokens_ref, x_all.at[chip, core], own_sem)
    own_copy.start()
    for step in range(steps):
        weight_copy(step).start()

    barrier = pltpu.get_barrier_semaphore()
    for k in range(1, tp_count):
        pl.semaphore_signal(
            barrier, inc=1, device_id={"tp": (tp + k) % tp_count}, device_id_type=MESH
        )
    for k in range(1, seq_count):
        pl.semaphore_signal(
            barrier, inc=1, device_id={"seq": (seq + k) % seq_count}, device_id_type=MESH
        )
    pl.semaphore_wait(barrier, tp_count - 1 + seq_count - 1)

    def send_tokens(c):
        for other in others:
            send(
                tokens_ref.at[rows_of(c)], x_all.at[chip, core, rows_of(c)],
                x_sem.at[chip, core, c], "tp", other * 2 + core,
            )

    for c in range(min(ahead, parts)):
        send_tokens(c)
    for c in range(parts):
        send(
            tokens_ref.at[rows_of(c)], x_all.at[chip, core, rows_of(c)],
            x_sem.at[chip, core, c], "tp", partner,
        )

    def compute(where, low, count, first):
        rows = pl.ds(low, count)
        x = x_all[where, :, rows, :].reshape(2 * count, width)
        mid_ref[pl.ds(0, 2 * count)] = lax.dot_general(
            x, down_ref[...], (((1,), (1,)), ((), ())), preferred_element_type=jnp.float32
        ).astype(jnp.bfloat16)

        @pl.loop(0, steps)
        def _(step):
            if first:
                weight_copy(step).wait()
            x = x_all[where, :, rows, :].reshape(2 * count, width)
            joined = jnp.dot(x, w_all[step], preferred_element_type=jnp.float32)
            joined = joined + ADAPTER_SCALE * jnp.dot(
                mid_ref[pl.ds(0, 2 * count)], up_ref[:, pl.ds(pl.multiple_of(step * wide, wide), wide)],
                preferred_element_type=jnp.float32
            )
            kind = step // rotated_pairs
            cosine = cos_ref[kind, where, :, rows, :].reshape(2 * count, DH)
            sine = sin_ref[kind, where, :, rows, :].reshape(2 * count, DH)
            for head in range(pair):
                piece = joined[:, head * DH : (head + 1) * DH]
                piece = piece * cosine + pltpu.roll(piece, DH // 2, 1) * sine
                piece = piece.astype(jnp.bfloat16)
                for k in range(2):
                    stage[where, k, step * pair + head, rows] = piece[k * count : (k + 1) * count]

    def give(where, k, c, target):
        send(
            stage.at[where, k, :, rows_of(c)], landed[c].at[tp], land_sem.at[tp, c], "tp", target
        )

    def hold(src, dst, sem):
        copy = pltpu.make_async_copy(src, dst, sem)
        copy.start()
        locals_.append(copy)

    def project(c):
        for other in others:
            block = x_all.at[other, core, rows_of(c)]
            arrived(block, x_sem.at[other, core, c], "tp", other * 2 + core)
            send(block, block, x_sem.at[other, core, c], "tp", partner)
        for other in others:
            arrived(
                x_all.at[other, 1 - core, rows_of(c)], x_sem.at[other, 1 - core, c], "tp", partner
            )
            compute(other, c * part, part, False)
            for k in range(2):
                give(other, k, c, other * 2 + k)
        if c + ahead < parts:
            send_tokens(c + ahead)

    def exchange(c):
        rows = rows_of(c)
        keeps[c].wait()
        for k in range(1, tp_count):
            source = (tp + k) % tp_count
            arrived(landed[c].at[source], land_sem.at[source, c], "tp", source)

        @pl.loop(0, seq_count)
        def _(j):
            kv_head = j * here // GROUP
            for k in range(2):
                sent[j, here + k, rows] = landed[c][
                    kv_head // kv_per, q_per + k * kv_per + kv_head % kv_per
                ]

        for j in near:
            send(
                sent.at[j, pl.ds(here, 2), rows], kv_ref.at[tp, seq, :, rows],
                kv_sem.at[seq, c], "seq", j,
            )
        hold(sent.at[seq, pl.ds(here, 2), rows], kv_ref.at[tp, seq, :, rows], hold_sem.at[0, c])

        @pl.loop(0, seq_count)
        def _(j):
            for k in range(here):
                head = index_ref[j * here + k]
                sent[j, k, rows] = landed[c][head // q_per, head % q_per]

        for j in near:
            send(
                sent.at[j, pl.ds(0, here), rows], q_ref.at[seq, :, rows],
                q_sem.at[seq, c], "seq", j,
            )
        hold(sent.at[seq, pl.ds(0, here), rows], q_ref.at[seq, :, rows], hold_sem.at[1, c])

    def spread(c):
        rows = rows_of(c)
        locals_[2 * c].wait()
        for source in near:
            arrived(kv_ref.at[tp, source, :, rows], kv_sem.at[source, c], "seq", source)
        block = kv_ref.at[tp, :, :, rows]
        for other in others:
            send(block, block, spread_sem.at[tp, c], "tp", other * 2 + core)
        send(block, block, spread_sem.at[tp, c], "tp", partner)

    def forward(c):
        for other in others:
            far = other * 2 + core
            block = kv_ref.at[far, :, :, rows_of(c)]
            arrived(block, spread_sem.at[far, c], "tp", far)
            send(block, block, spread_sem.at[far, c], "tp", partner)

    own_copy.wait()
    for c in range(parts):
        arrived(x_all.at[chip, 1 - core, rows_of(c)], x_sem.at[chip, 1 - core, c], "tp", partner)
    compute(chip, 0, own, True)
    keeps = [
        pltpu.make_async_copy(
            stage.at[chip, core, :, rows_of(c)], landed[c].at[tp], keep_sem.at[c]
        )
        for c in range(parts)
    ]
    for c in range(parts):
        keeps[c].start()
        give(chip, 1 - core, c, partner)

    for step in range(parts + 3):
        if step < parts:
            project(step)
        if 0 <= step - 1 < parts:
            exchange(step - 1)
        if 0 <= step - 2 < parts:
            spread(step - 2)
        if 0 <= step - 3 < parts:
            forward(step - 3)

    for c in range(parts):
        rows = rows_of(c)
        locals_[2 * c + 1].wait()
        for source in near:
            arrived(q_ref.at[source, :, rows], q_sem.at[source, c], "seq", source)
        for k in range(chips):
            source = (chip + k) % chips * 2 + 1 - core
            arrived(kv_ref.at[source, :, :, rows], spread_sem.at[source, c], "tp", partner)
    for copy in sends:
        copy.wait_send()


PARTS = 4
AHEAD = 2


def front(index, tokens, w, down, up, cosine, sine, tp_count, seq_count, rotated_heads):
    own, width = tokens.shape
    heads = w.shape[1] // DH
    pair = 2
    steps = heads // pair
    chips = tp_count // 2
    here = H // seq_count
    rank = down.shape[1]
    parts = PARTS
    vmem = pl.BlockSpec(memory_space=pltpu.VMEM)
    anywhere = pl.BlockSpec(memory_space=pl.ANY)
    tokens_out = parts * (2 * (chips - 1) + 1)
    results_out = parts * (2 * (chips - 1) + 1)
    spread_out = parts * (2 * (chips - 1) + 1)
    count = tokens_out + results_out + spread_out + 2 * parts * (seq_count - 1)
    bf16 = jnp.bfloat16
    dma = pltpu.SemaphoreType.DMA
    return pl.pallas_call(
        functools.partial(front_kernel, rotated_heads // pair, here, AHEAD),
        in_specs=[pl.BlockSpec(memory_space=pltpu.SMEM), anywhere, anywhere, vmem, vmem, vmem, vmem],
        out_specs=[anywhere, anywhere],
        out_shape=[
            jax.ShapeDtypeStruct((seq_count, here, own, DH), bf16),
            jax.ShapeDtypeStruct((tp_count, seq_count, 2, own, DH), bf16),
        ],
        scratch_shapes=[
            pltpu.VMEM((chips, 2, own, width), bf16),
            pltpu.VMEM((steps, width, pair * DH), bf16),
            pltpu.VMEM((chips, 2, heads, own, DH), bf16),
            pltpu.VMEM((seq_count, here + 2, own, DH), bf16),
            pltpu.VMEM((2 * own, rank), bf16),
            dma((steps,)),
            dma(()),
            dma((parts,)),
            dma((2, parts)),
            dma((count,)),
            dma((chips, 2, parts)),
            dma((tp_count, parts)),
            dma((seq_count, parts)),
            dma((seq_count, parts)),
            dma((tp_count, parts)),
        ]
        + [pltpu.VMEM((tp_count, heads, own // parts, DH), bf16)] * parts,
        compiler_params=pltpu.CompilerParams(collective_id=0, has_side_effects=True),
        name="front",
    )(index, tokens, w, down.T, up, cosine, sine)


def tail_kernel(
    slot_ref, q_hbm, kv_hbm, doc_ref, out_ref,
    q_ref, kv_ref, context, landed, send_sem, land_sem, local_sem,
):
    tp = lax.axis_index("tp")
    seq = lax.axis_index("seq")
    seq_count, heads, own, _ = q_ref.shape
    chunks = kv_ref.shape[0]
    block = chunks * own
    rows = heads * own
    loads = [
        pltpu.make_async_copy(q_hbm, q_ref, local_sem.at[0]),
        pltpu.make_async_copy(kv_hbm, kv_ref, local_sem.at[1]),
    ]
    for load in loads:
        load.start()
    barrier = pltpu.get_barrier_semaphore()
    for k in range(1, seq_count):
        pl.semaphore_signal(
            barrier, inc=1, device_id={"seq": (seq + k) % seq_count}, device_id_type=MESH
        )
    pl.semaphore_wait(barrier, seq_count - 1)
    for load in loads:
        load.wait()
    factor = (DH**-0.5) * LOG2_E

    def toggled(change):
        result, bit = 0, 1
        while bit < seq_count:
            mine, flip = seq // bit % 2, change // bit % 2
            result = result + bit * (mine + flip - 2 * mine * flip)
            bit *= 2
        return result

    def attend(step):
        q = q_ref[step].reshape(rows, DH)
        docs = doc_ref[pl.ds(step * chunks + tp, 1), :]
        docs = jnp.broadcast_to(docs, (own, own)).T[:, :1]
        docs = jnp.concatenate([docs] * heads, 0)
        places = tp * own + lax.broadcasted_iota(jnp.int32, (own, 1), 0)
        places = jnp.concatenate([places] * heads, 0)

        def body(index, carry, own_block=False):
            top, total, acc = carry
            keys = kv_ref[:, index, 0].reshape(block, DH)
            values = kv_ref[:, index, 1].reshape(block, DH)
            scores = lax.dot_general(
                q, keys, (((1,), (1,)), ((), ())), preferred_element_type=jnp.float32
            )
            key_docs = jnp.concatenate(
                [doc_ref[pl.ds(index * chunks + c, 1), :] for c in range(chunks)], 1
            )
            kept = key_docs == docs
            if own_block:
                kept = kept & (lax.broadcasted_iota(jnp.int32, (1, block), 1) <= places)
            scores = jnp.where(kept, scores, NEG_BIG)
            new_top = jnp.maximum(top, jnp.max(scores, 1, keepdims=True))
            shrink = jnp.exp2((top - new_top) * factor)
            powers = jnp.exp2((scores - new_top) * factor)
            total = total * shrink + jnp.sum(powers, 1, keepdims=True)
            acc = acc * shrink + jnp.dot(
                powers.astype(jnp.bfloat16), values, preferred_element_type=jnp.float32
            )
            return new_top, total, acc

        start = (
            jnp.full((rows, 1), NEG_BIG, jnp.float32),
            jnp.zeros((rows, 1), jnp.float32),
            jnp.zeros((rows, DH), jnp.float32),
        )
        _, total, acc = lax.fori_loop(0, step, body, body(step, start, True))
        return (acc / total).astype(jnp.bfloat16).reshape(heads, own, DH)

    def outgoing(change):
        target = toggled(change)
        return target, pltpu.make_async_remote_copy(
            src_ref=context.at[change], dst_ref=landed.at[seq], send_sem=send_sem.at[change],
            recv_sem=land_sem.at[seq], device_id={"seq": target}, device_id_type=MESH,
        )

    def give(change):
        target, copy = outgoing(change)
        context[change] = attend(target)
        copy.start()

    half = seq_count // 2

    @pl.loop(0, half)
    def _(i):
        give(half + i)

    @pl.loop(0, half - 1)
    def _(i):
        give(half - 1 - i)

    landed[seq] = attend(seq)

    @pl.loop(1, seq_count)
    def _(change):
        source = toggled(change)
        pltpu.make_async_remote_copy(
            src_ref=landed.at[source], dst_ref=landed.at[source], send_sem=send_sem.at[0],
            recv_sem=land_sem.at[source], device_id={"seq": source}, device_id_type=MESH,
        ).wait_recv()

    for head in range(seq_count * heads):
        slot = slot_ref[head]
        out_ref[:, head * DH : (head + 1) * DH] = landed[slot // heads, slot % heads]

    @pl.loop(1, seq_count)
    def _(change):
        outgoing(change)[1].wait_send()


def tail(slot, q, kv, document_index):
    seq_count, heads, own, _ = q.shape
    vmem = pl.BlockSpec(memory_space=pltpu.VMEM)
    anywhere = pl.BlockSpec(memory_space=pl.ANY)
    return pl.pallas_call(
        tail_kernel,
        in_specs=[pl.BlockSpec(memory_space=pltpu.SMEM), anywhere, anywhere, vmem],
        out_specs=vmem,
        out_shape=jax.ShapeDtypeStruct((own, seq_count * heads * DH), q.dtype),
        scratch_shapes=[
            pltpu.VMEM(q.shape, q.dtype),
            pltpu.VMEM(kv.shape, kv.dtype),
            pltpu.VMEM(q.shape, q.dtype),
            pltpu.VMEM(q.shape, q.dtype),
            pltpu.SemaphoreType.DMA((seq_count,)),
            pltpu.SemaphoreType.DMA((seq_count,)),
            pltpu.SemaphoreType.DMA((2,)),
        ],
        compiler_params=pltpu.CompilerParams(collective_id=1, has_side_effects=True),
        name="tail",
    )(slot, q, kv, document_index.reshape(-1, own))


def head_tables(query_to_key_head):
    heads = jnp.arange(H, dtype=jnp.int32)
    same = query_to_key_head[:, None] == query_to_key_head[None, :]
    earlier = heads[None, :] < heads[:, None]
    slot = GROUP * query_to_key_head + jnp.sum((same & earlier).astype(jnp.int32), 1)
    order = jnp.sum(jnp.where(slot[None, :] == heads[:, None], heads[None, :], 0), 1)
    return order.astype(jnp.int32), slot.astype(jnp.int32)


def per_device(
    tokens,
    joined_projection_weight,
    adapter_down_weight,
    adapter_up_weight,
    document_index,
    query_to_key_head,
):
    tp_count = lax.axis_size("tp")
    seq_count = lax.axis_size("seq")
    tp_rank = lax.axis_index("tp")
    seq_rank = lax.axis_index("seq")
    own = tokens.shape[0]
    block = own * tp_count
    here = H // seq_count
    q_per, kv_per = H // tp_count, KV // tp_count

    index, slot = head_tables(query_to_key_head)
    places = (seq_rank * block + jnp.arange(block, dtype=jnp.int32)).astype(jnp.float32)
    cosine, sine = rope_tables(places)
    table = (1, tp_count // 2, 2, own, DH)
    cosine = jnp.concatenate([cosine.reshape(table), jnp.ones(table, jnp.float32)])
    sine = jnp.concatenate([sine.reshape(table), jnp.zeros(table, jnp.float32)])
    held, kv = front(
        index, tokens, joined_projection_weight, adapter_down_weight, adapter_up_weight,
        cosine, sine, tp_count, seq_count, q_per + kv_per,
    )
    return tail(slot, held, kv, document_index)


def solution(mesh):
    return jax.shard_map(
        per_device,
        mesh=mesh,
        in_specs=(P(("seq", "tp"), None), P(None, "tp"), P(), P(None, "tp"), P(), P()),
        out_specs=P(("seq", "tp"), None),
        check_vma=False,
    )
```

time: 126 us -> 114 us (0.905)
  Pallas kernels: 118 us -> 105 us
    pallas_call x2 -> x1, Pallas kernels: 45 us -> 34.8 us  [tail(): pl.pallas_call(tail_kernel, in_specs=[pl.BlockSpec(memory_space=pltpu.SME...]
    pallas_call x1, Pallas kernels: 72.5 us -> 70.1 us  [front(): pl.pallas_call(functools.partial(front_kernel, rotated_heads // pair, her...]
where the time goes in v2:
time: 114 us; the launch traced here: 112 us
  Pallas kernels  105 us (92%)
  other arithmetic  4.38 us (4%)
  local copies, waits for them, and re-layouts  2.29 us (2%)
    pallas_call x1, Pallas kernels, front(): pl.pallas_call(functools.partial(front_kernel, rotated_heads // pair, her...  70.1 us
    pallas_call x1, Pallas kernels, tail(): pl.pallas_call(tail_kernel, in_specs=[pl.BlockSpec(memory_space=pltpu.SME...  34.8 us
    unnamed x3, local copies, waits for them, and re-layouts  2.29 us

profile of v2, /device:TPU:13, one launch (start us, length us, event | category | flops | bytes accessed | tf_op | source)
XLA Modules:
  0.0 111.6 jit_solution(15261408775755596280)
XLA Ops:
  0.0 0.9 convert_reduce_fusion
  0.9 0.7 multiply_add_fusion.slot_ref
  1.6 0.0 copy-start
  1.6 0.6 select_reduce_fusion.index_ref
  2.2 1.0 fusion
  3.2 1.2 %select_maximum_fusion = (f32[2,2,2,128,128]{4,3,2,1,0:T(8,128)}, f32[2,2,2,128,128]{4,3,2,1,0:T(8,128)}) fusion(f32[1,2,2,128,64]{4,3,2,1,0:T(8,128)S(1)} %get-tuple-element.10, f32[1,2,2,128,64]{4,3,2,1,0:T(8,128)S(1)} %get-tuple-element.9, f32[1,2,2,128,64]{4,3,2,1,0:T(8,128)S(1)} %get-tuple-element.11), kind=kLoop, calls=%fused_computation | loop fusion | flops 917504 | bytes 1441792 | tf_op jit(solution)/shard_map/concatenate | solution.py:26
  4.4 70.1 %front.1 = (bf16[8,4,128,128]{3,2,1,0:T(8,128)(2,1)}, bf16[4,8,2,128,128]{4,3,2,1,0:T(8,128)(2,1)}) custom-call(s32[32]{0:T(128)} %select_reduce_fusion.index_ref, bf16[128,4096]{1,0:T(8,128)(2,1)} %tokens_ref.1, bf16[4096,1536]{1,0:T(8,128)(2,1)} %w_ref.1, bf16[64,4096]{1,0:T(8,128)(2,1)} %bitcast.2, bf16[64,1536]{1,0:T(8,128)(2,1)} %up_ref.1, ...), custom_call_target="tpu_custom_call" | custom-call | tf_op jit(solution)/shard_map/front/pallas_call | solution.py:270
  74.5 0.0 copy-done
  74.5 34.8 %tail.1 = bf16[128,4096]{1,0:T(8,128)(2,1)} custom-call(s32[32]{0:T(128)} %copy-done, bf16[8,4,128,128]{3,2,1,0:T(8,128)(2,1)} %get-tuple-element.7.q_hbm, bf16[4,8,2,128,128]{4,3,2,1,0:T(8,128)(2,1)} %get-tuple-element.8.kv_hbm, s32[32,128]{1,0:T(8,128)} %bitcast.3), custom_call_target="tpu_custom_call" | custom-call | tf_op jit(solution)/shard_map/tail/pallas_call | solution.py:419
  109.4 2.3 %copy.8 = bf16[128,4096]{1,0:T(8,128)(2,1)} copy(bf16[128,4096]{1,0:T(8,128)(2,1)} %tail.1) | data formatting | bytes 2097152
  (2 shorter events, 0.0 us)
Async XLA Ops:
  1.6 72.9 %copy-start = (s32[32]{0:T(128)}, s32[32]{0:T(128)S(1)}, u32[]{:S(2)}) copy-start(s32[32]{0:T(128)S(1)} %multiply_add_fusion.slot_ref) | copy-start | bytes 388

commit v3 on v2

--- a/solution.py
+++ b/solution.py
@@ -29,12 +29,12 @@
 MESH = pl.DeviceIdType.MESH
 
 
-def front_kernel(
-    rotated_pairs, here, ahead, index_ref, tokens_ref, w_ref, down_ref, up_ref, cos_ref, sin_ref,
-    q_ref, kv_ref,
-    x_all, w_all, stage, sent, mid_ref,
+def layer_kernel(
+    rotated_pairs, here, ahead, index_ref, slot_ref, doc_ref,
+    tokens_ref, w_ref, down_ref, up_ref, cos_ref, sin_ref, out_ref,
+    x_all, w_all, stage, sent, mid_ref, q_ref, kv_ref, context, final,
     w_sem, own_sem, keep_sem, hold_sem, send_sem, x_sem, land_sem, q_sem, kv_sem, spread_sem,
-    *landed,
+    give_sem, final_sem, *landed,
 ):
     tp = lax.axis_index("tp")
     seq = lax.axis_index("seq")
@@ -235,13 +235,103 @@
             forward(step - 3)
 
     for c in range(parts):
-        rows = rows_of(c)
         locals_[2 * c + 1].wait()
-        for source in near:
-            arrived(q_ref.at[source, :, rows], q_sem.at[source, c], "seq", source)
         for k in range(chips):
             source = (chip + k) % chips * 2 + 1 - core
-            arrived(kv_ref.at[source, :, :, rows], spread_sem.at[source, c], "tp", partner)
+            arrived(kv_ref.at[source, :, :, rows_of(c)], spread_sem.at[source, c], "tp", partner)
+
+    block = tp_count * own
+    rows = here * own
+    factor = (DH**-0.5) * LOG2_E
+
+    def toggled(change):
+        result, bit = 0, 1
+        while bit < seq_count:
+            mine, flip = seq // bit % 2, change // bit % 2
+            result = result + bit * (mine + flip - 2 * mine * flip)
+            bit *= 2
+        return result
+
+    def attend(step):
+        q = q_ref[step].reshape(rows, DH)
+        docs = doc_ref[pl.ds(step * tp_count + tp, 1), :]
+        docs = jnp.broadcast_to(docs, (own, own)).T[:, :1]
+        docs = jnp.concatenate([docs] * here, 0)
+        places = tp * own + lax.broadcasted_iota(jnp.int32, (own, 1), 0)
+        places = jnp.concatenate([places] * here, 0)
+
+        def body(index, carry, own_block=False):
+            top, total, acc = carry
+            keys = kv_ref[:, index, 0].reshape(block, DH)
+            values = kv_ref[:, index, 1].reshape(block, DH)
+            scores = lax.dot_general(
+                q, keys, (((1,), (1,)), ((), ())), preferred_element_type=jnp.float32
+            )
+            key_docs = jnp.concatenate(
+                [doc_ref[pl.ds(index * tp_count + c, 1), :] for c in range(tp_count)], 1
+            )
+            kept = key_docs == docs
+            if own_block:
+                kept = kept & (lax.broadcasted_iota(jnp.int32, (1, block), 1) <= places)
+            scores = jnp.where(kept, scores, NEG_BIG)
+            new_top = jnp.maximum(top, jnp.max(scores, 1, keepdims=True))
+            shrink = jnp.exp2((top - new_top) * factor)
+            powers = jnp.exp2((scores - new_top) * factor)
+            total = total * shrink + jnp.sum(powers, 1, keepdims=True)
+            acc = acc * shrink + jnp.dot(
+                powers.astype(jnp.bfloat16), values, preferred_element_type=jnp.float32
+            )
+            return new_top, total, acc
+
+        start = (
+            jnp.full((rows, 1), NEG_BIG, jnp.float32),
+            jnp.zeros((rows, 1), jnp.float32),
+            jnp.zeros((rows, DH), jnp.float32),
+        )
+        _, total, acc = lax.fori_loop(0, step, body, body(step, start, True))
+        return (acc / total).astype(jnp.bfloat16).reshape(here, own, DH)
+
+    def outgoing(change):
+        target = toggled(change)
+        return target, pltpu.make_async_remote_copy(
+            src_ref=context.at[change], dst_ref=final.at[seq], send_sem=give_sem.at[change],
+            recv_sem=final_sem.at[seq], device_id={"seq": target}, device_id_type=MESH,
+        )
+
+    def hand(change):
+        target, copy = outgoing(change)
+        for c in range(parts):
+            arrived(q_ref.at[target, :, rows_of(c)], q_sem.at[target, c], "seq", target)
+        context[change] = attend(target)
+        copy.start()
+
+    half = seq_count // 2
+
+    @pl.loop(0, half)
+    def _(i):
+        hand(half + i)
+
+    @pl.loop(0, half - 1)
+    def _(i):
+        hand(half - 1 - i)
+
+    final[seq] = attend(seq)
+
+    @pl.loop(1, seq_count)
+    def _(change):
+        source = toggled(change)
+        pltpu.make_async_remote_copy(
+            src_ref=final.at[source], dst_ref=final.at[source], send_sem=give_sem.at[0],
+            recv_sem=final_sem.at[source], device_id={"seq": source}, device_id_type=MESH,
+        ).wait_recv()
+
+    for head in range(seq_count * here):
+        slot = slot_ref[head]
+        out_ref[:, head * DH : (head + 1) * DH] = final[slot // here, slot % here]
+
+    @pl.loop(1, seq_count)
+    def _(change):
+        outgoing(change)[1].wait_send()
     for copy in sends:
         copy.wait_send()
 
@@ -250,7 +340,10 @@
 AHEAD = 2
 
 
-def front(index, tokens, w, down, up, cosine, sine, tp_count, seq_count, rotated_heads):
+def layer(
+    index, slot, document_index, tokens, w, down, up, cosine, sine, tp_count, seq_count,
+    rotated_heads,
+):
     own, width = tokens.shape
     heads = w.shape[1] // DH
     pair = 2
@@ -260,27 +353,27 @@
     rank = down.shape[1]
     parts = PARTS
     vmem = pl.BlockSpec(memory_space=pltpu.VMEM)
+    smem = pl.BlockSpec(memory_space=pltpu.SMEM)
     anywhere = pl.BlockSpec(memory_space=pl.ANY)
-    tokens_out = parts * (2 * (chips - 1) + 1)
-    results_out = parts * (2 * (chips - 1) + 1)
-    spread_out = parts * (2 * (chips - 1) + 1)
-    count = tokens_out + results_out + spread_out + 2 * parts * (seq_count - 1)
+    count = 3 * parts * (2 * (chips - 1) + 1) + 2 * parts * (seq_count - 1)
     bf16 = jnp.bfloat16
     dma = pltpu.SemaphoreType.DMA
+    mine = (seq_count, here, own, DH)
     return pl.pallas_call(
-        functools.partial(front_kernel, rotated_heads // pair, here, AHEAD),
-        in_specs=[pl.BlockSpec(memory_space=pltpu.SMEM), anywhere, anywhere, vmem, vmem, vmem, vmem],
-        out_specs=[anywhere, anywhere],
-        out_shape=[
-            jax.ShapeDtypeStruct((seq_count, here, own, DH), bf16),
-            jax.ShapeDtypeStruct((tp_count, seq_count, 2, own, DH), bf16),
-        ],
+        functools.partial(layer_kernel, rotated_heads // pair, here, AHEAD),
+        in_specs=[smem, smem, vmem, anywhere, anywhere, vmem, vmem, vmem, vmem],
+        out_specs=vmem,
+        out_shape=jax.ShapeDtypeStruct((own, H * DH), bf16),
         scratch_shapes=[
             pltpu.VMEM((chips, 2, own, width), bf16),
             pltpu.VMEM((steps, width, pair * DH), bf16),
             pltpu.VMEM((chips, 2, heads, own, DH), bf16),
             pltpu.VMEM((seq_count, here + 2, own, DH), bf16),
             pltpu.VMEM((2 * own, rank), bf16),
+            pltpu.VMEM(mine, bf16),
+            pltpu.VMEM((tp_count, seq_count, 2, own, DH), bf16),
+            pltpu.VMEM(mine, bf16),
+            pltpu.VMEM(mine, bf16),
             dma((steps,)),
             dma(()),
             dma((parts,)),
@@ -291,148 +384,15 @@
             dma((seq_count, parts)),
             dma((seq_count, parts)),
             dma((tp_count, parts)),
+            dma((seq_count,)),
+            dma((seq_count,)),
         ]
         + [pltpu.VMEM((tp_count, heads, own // parts, DH), bf16)] * parts,
         compiler_params=pltpu.CompilerParams(collective_id=0, has_side_effects=True),
-        name="front",
-    )(index, tokens, w, down.T, up, cosine, sine)
-
-
-def tail_kernel(
-    slot_ref, q_hbm, kv_hbm, doc_ref, out_ref,
-    q_ref, kv_ref, context, landed, send_sem, land_sem, local_sem,
-):
-    tp = lax.axis_index("tp")
-    seq = lax.axis_index("seq")
-    seq_count, heads, own, _ = q_ref.shape
-    chunks = kv_ref.shape[0]
-    block = chunks * own
-    rows = heads * own
-    loads = [
-        pltpu.make_async_copy(q_hbm, q_ref, local_sem.at[0]),
-        pltpu.make_async_copy(kv_hbm, kv_ref, local_sem.at[1]),
-    ]
-    for load in loads:
-        load.start()
-    barrier = pltpu.get_barrier_semaphore()
-    for k in range(1, seq_count):
-        pl.semaphore_signal(
-            barrier, inc=1, device_id={"seq": (seq + k) % seq_count}, device_id_type=MESH
-        )
-    pl.semaphore_wait(barrier, seq_count - 1)
-    for load in loads:
-        load.wait()
-    factor = (DH**-0.5) * LOG2_E
-
-    def toggled(change):
-        result, bit = 0, 1
-        while bit < seq_count:
-            mine, flip = seq // bit % 2, change // bit % 2
-            result = result + bit * (mine + flip - 2 * mine * flip)
-            bit *= 2
-        return result
-
-    def attend(step):
-        q = q_ref[step].reshape(rows, DH)
-        docs = doc_ref[pl.ds(step * chunks + tp, 1), :]
-        docs = jnp.broadcast_to(docs, (own, own)).T[:, :1]
-        docs = jnp.concatenate([docs] * heads, 0)
-        places = tp * own + lax.broadcasted_iota(jnp.int32, (own, 1), 0)
-        places = jnp.concatenate([places] * heads, 0)
-
-        def body(index, carry, own_block=False):
-            top, total, acc = carry
-            keys = kv_ref[:, index, 0].reshape(block, DH)
-            values = kv_ref[:, index, 1].reshape(block, DH)
-            scores = lax.dot_general(
-                q, keys, (((1,), (1,)), ((), ())), preferred_element_type=jnp.float32
-            )
-            key_docs = jnp.concatenate(
-                [doc_ref[pl.ds(index * chunks + c, 1), :] for c in range(chunks)], 1
-            )
-            kept = key_docs == docs
-            if own_block:
-                kept = kept & (lax.broadcasted_iota(jnp.int32, (1, block), 1) <= places)
-            scores = jnp.where(kept, scores, NEG_BIG)
-            new_top = jnp.maximum(top, jnp.max(scores, 1, keepdims=True))
-            shrink = jnp.exp2((top - new_top) * factor)
-            powers = jnp.exp2((scores - new_top) * factor)
-            total = total * shrink + jnp.sum(powers, 1, keepdims=True)
-            acc = acc * shrink + jnp.dot(
-                powers.astype(jnp.bfloat16), values, preferred_element_type=jnp.float32
-            )
-            return new_top, total, acc
-
-        start = (
-            jnp.full((rows, 1), NEG_BIG, jnp.float32),
-            jnp.zeros((rows, 1), jnp.float32),
-            jnp.zeros((rows, DH), jnp.float32),
-        )
-        _, total, acc = lax.fori_loop(0, step, body, body(step, start, True))
-        return (acc / total).astype(jnp.bfloat16).reshape(heads, own, DH)
-
-    def outgoing(change):
-        target = toggled(change)
-        return target, pltpu.make_async_remote_copy(
-            src_ref=context.at[change], dst_ref=landed.at[seq], send_sem=send_sem.at[change],
-            recv_sem=land_sem.at[seq], device_id={"seq": target}, device_id_type=MESH,
-        )
-
-    def give(change):
-        target, copy = outgoing(change)
-        context[change] = attend(target)
-        copy.start()
-
-    half = seq_count // 2
-
-    @pl.loop(0, half)
-    def _(i):
-        give(half + i)
-
-    @pl.loop(0, half - 1)
-    def _(i):
-        give(half - 1 - i)
-
-    landed[seq] = attend(seq)
-
-    @pl.loop(1, seq_count)
-    def _(change):
-        source = toggled(change)
-        pltpu.make_async_remote_copy(
-            src_ref=landed.at[source], dst_ref=landed.at[source], send_sem=send_sem.at[0],
-            recv_sem=land_sem.at[source], device_id={"seq": source}, device_id_type=MESH,
-        ).wait_recv()
-
-    for head in range(seq_count * heads):
-        slot = slot_ref[head]
-        out_ref[:, head * DH : (head + 1) * DH] = landed[slot // heads, slot % heads]
-
-    @pl.loop(1, seq_count)
-    def _(change):
-        outgoing(change)[1].wait_send()
-
-
-def tail(slot, q, kv, document_index):
-    seq_count, heads, own, _ = q.shape
-    vmem = pl.BlockSpec(memory_space=pltpu.VMEM)
-    anywhere = pl.BlockSpec(memory_space=pl.ANY)
-    return pl.pallas_call(
-        tail_kernel,
-        in_specs=[pl.BlockSpec(memory_space=pltpu.SMEM), anywhere, anywhere, vmem],
-        out_specs=vmem,
-        out_shape=jax.ShapeDtypeStruct((own, seq_count * heads * DH), q.dtype),
-        scratch_shapes=[
-            pltpu.VMEM(q.shape, q.dtype),
-            pltpu.VMEM(kv.shape, kv.dtype),
-            pltpu.VMEM(q.shape, q.dtype),
-            pltpu.VMEM(q.shape, q.dtype),
-            pltpu.SemaphoreType.DMA((seq_count,)),
-            pltpu.SemaphoreType.DMA((seq_count,)),
-            pltpu.SemaphoreType.DMA((2,)),
-        ],
-        compiler_params=pltpu.CompilerParams(collective_id=1, has_side_effects=True),
-        name="tail",
-    )(slot, q, kv, document_index.reshape(-1, own))
+        name="layer",
+    )(
+        index, slot, document_index.reshape(-1, own), tokens, w, down.T, up, cosine, sine,
+    )
 
 
 def head_tables(query_to_key_head):
@@ -467,11 +427,10 @@
     table = (1, tp_count // 2, 2, own, DH)
     cosine = jnp.concatenate([cosine.reshape(table), jnp.ones(table, jnp.float32)])
     sine = jnp.concatenate([sine.reshape(table), jnp.zeros(table, jnp.float32)])
-    held, kv = front(
-        index, tokens, joined_projection_weight, adapter_down_weight, adapter_up_weight,
-        cosine, sine, tp_count, seq_count, q_per + kv_per,
+    return layer(
+        index, slot, document_index, tokens, joined_projection_weight, adapter_down_weight,
+        adapter_up_weight, cosine, sine, tp_count, seq_count, q_per + kv_per,
     )
-    return tail(slot, held, kv, document_index)
 
 
 def solution(mesh):

time: 114 us -> 108 us (0.947); the launches traced: 112 us -> 107 us
  Pallas kernels: 105 us -> 101 us
    pallas_call x2 -> x1, Pallas kernels: 105 us -> 101 us  [layer(): pl.pallas_call(functools.partial(layer_kernel, rotated_heads // pair, her...]
where the time goes in v3:
time: 108 us; the launch traced here: 107 us
  Pallas kernels  101 us (94%)
  other arithmetic  4.44 us (4%)
  local copies, waits for them, and re-layouts  2.29 us (2%)
    pallas_call x1, Pallas kernels, layer(): pl.pallas_call(functools.partial(layer_kernel, rotated_heads // pair, her...  101 us
    unnamed x3, local copies, waits for them, and re-layouts  2.29 us

profile of v3, /device:TPU:13, one launch (start us, length us, event | category | flops | bytes accessed | tf_op | source)
XLA Modules:
  0.0 107.3 jit_solution(15479351711983859881)
XLA Ops:
  0.0 0.9 convert_reduce_fusion
  0.9 0.7 multiply_add_fusion.slot_ref
  1.6 0.0 copy-start
  1.6 0.7 select_reduce_fusion.index_ref
  2.3 1.0 fusion
  3.3 1.2 %select_maximum_fusion = (f32[2,2,2,128,128]{4,3,2,1,0:T(8,128)}, f32[2,2,2,128,128]{4,3,2,1,0:T(8,128)}) fusion(f32[1,2,2,128,64]{4,3,2,1,0:T(8,128)S(1)} %get-tuple-element.6, f32[1,2,2,128,64]{4,3,2,1,0:T(8,128)S(1)} %get-tuple-element.5, f32[1,2,2,128,64]{4,3,2,1,0:T(8,128)S(1)} %get-tuple-element.7), kind=kLoop, calls=%fused_computation | loop fusion | flops 917504 | bytes 1441792 | tf_op jit(solution)/shard_map/concatenate | solution.py:26
  4.5 0.0 copy-done
  4.5 100.6 %layer.1 = bf16[128,4096]{1,0:T(8,128)(2,1)} custom-call(s32[32]{0:T(128)} %select_reduce_fusion.index_ref, s32[32]{0:T(128)} %copy-done, s32[32,128]{1,0:T(8,128)} %bitcast.3, bf16[128,4096]{1,0:T(8,128)(2,1)} %tokens_ref.1, bf16[4096,1536]{1,0:T(8,128)(2,1)} %w_ref.1, bf16[64,4096]{1,0:T(8,128)(2,1)} %bitcast.2, bf16[64,1536]{1,0:T(8,128)(2,1)} %up_ref.1, ...), custom_call_target="tpu_custom_call" | custom-call | tf_op jit(solution)/shard_map/layer/pallas_call | solution.py:362
  105.0 2.3 %copy.8 = bf16[128,4096]{1,0:T(8,128)(2,1)} copy(bf16[128,4096]{1,0:T(8,128)(2,1)} %layer.1) | data formatting | bytes 2097152
  (2 shorter events, 0.0 us)
Async XLA Ops:
  1.6 2.9 %copy-start = (s32[32]{0:T(128)}, s32[32]{0:T(128)S(1)}, u32[]{:S(2)}) copy-start(s32[32]{0:T(128)S(1)} %multiply_add_fusion.slot_ref) | copy-start | bytes 388

commit v4 on v3

--- a/solution.py
+++ b/solution.py
@@ -18,23 +18,16 @@
 LOG2_E = 1.4426950408889634
 
 
-def rope_tables(places):
-    half = DH // 2
-    frequency = THETA ** (-(jnp.arange(half, dtype=jnp.float32) * 2.0) / DH)
-    angles = places[:, None] * frequency[None, :]
-    cosine, sine = jnp.cos(angles), jnp.sin(angles)
-    return jnp.concatenate([cosine, cosine], 1), jnp.concatenate([-sine, sine], 1)
-
-
 MESH = pl.DeviceIdType.MESH
 
 
 def layer_kernel(
-    rotated_pairs, here, ahead, index_ref, slot_ref, doc_ref,
-    tokens_ref, w_ref, down_ref, up_ref, cos_ref, sin_ref, out_ref,
-    x_all, w_all, stage, sent, mid_ref, q_ref, kv_ref, context, final,
+    rotated, here, ahead, choice_ref, doc_ref, frequency_ref, tokens_ref, w_ref, down_ref, up_ref,
+    out_ref,
+    x_all, w_all, stage, sent, mid_ref, q_ref, kv_ref, context, final, cos_ref, sin_ref,
+    tables, slot_ref, index_ref,
     w_sem, own_sem, keep_sem, hold_sem, send_sem, x_sem, land_sem, q_sem, kv_sem, spread_sem,
-    give_sem, final_sem, *landed,
+    give_sem, final_sem, kv_send_sem, table_sem, *landed,
 ):
     tp = lax.axis_index("tp")
     seq = lax.axis_index("seq")
@@ -43,7 +36,7 @@
     tp_count, seq_count = 2 * chips, q_ref.shape[0]
     steps = w_all.shape[0]
     wide = w_all.shape[2]
-    pair = wide // DH
+    group = wide // DH
     chip, core = tp // 2, tp % 2
     partner = chip * 2 + (1 - core)
     others = [(chip + k) % chips for k in range(1, chips)]
@@ -106,32 +99,68 @@
             x_sem.at[chip, core, c], "tp", partner,
         )
 
-    def compute(where, low, count, first):
-        rows = pl.ds(low, count)
-        x = x_all[where, :, rows, :].reshape(2 * count, width)
-        mid_ref[pl.ds(0, 2 * count)] = lax.dot_general(
-            x, down_ref[...], (((1,), (1,)), ((), ())), preferred_element_type=jnp.float32
+    def compute(c):
+        rows = rows_of(c)
+        count = 2 * chips * part
+        mid_ref[...] = lax.dot_general(
+            x_all[:, :, rows, :].reshape(count, width), down_ref[...], (((1,), (1,)), ((), ())),
+            preferred_element_type=jnp.float32,
         ).astype(jnp.bfloat16)
 
         @pl.loop(0, steps)
         def _(step):
-            if first:
+            if c == 0:
                 weight_copy(step).wait()
-            x = x_all[where, :, rows, :].reshape(2 * count, width)
-            joined = jnp.dot(x, w_all[step], preferred_element_type=jnp.float32)
+            joined = jnp.dot(
+                x_all[:, :, rows, :].reshape(count, width), w_all[step],
+                preferred_element_type=jnp.float32,
+            )
             joined = joined + ADAPTER_SCALE * jnp.dot(
-                mid_ref[pl.ds(0, 2 * count)], up_ref[:, pl.ds(pl.multiple_of(step * wide, wide), wide)],
+                mid_ref[...], up_ref[:, pl.ds(pl.multiple_of(step * wide, wide), wide)],
                 preferred_element_type=jnp.float32
             )
-            kind = step // rotated_pairs
-            cosine = cos_ref[kind, where, :, rows, :].reshape(2 * count, DH)
-            sine = sin_ref[kind, where, :, rows, :].reshape(2 * count, DH)
-            for head in range(pair):
-                piece = joined[:, head * DH : (head + 1) * DH]
+            for n in range(group):
+                head = step * group + n
+                kind = head // rotated
+                cosine = cos_ref[kind, :, rows, :].reshape(count, DH)
+                sine = sin_ref[kind, :, rows, :].reshape(count, DH)
+                piece = joined[:, n * DH : (n + 1) * DH]
                 piece = piece * cosine + pltpu.roll(piece, DH // 2, 1) * sine
                 piece = piece.astype(jnp.bfloat16)
-                for k in range(2):
-                    stage[where, k, step * pair + head, rows] = piece[k * count : (k + 1) * count]
+                for place in range(2 * chips):
+                    stage[place // 2, place % 2, head, rows] = piece[
+                        place * part : (place + 1) * part
+                    ]
+
+    def make_tables():
+        for place in range(2 * chips):
+            row = lax.broadcasted_iota(jnp.int32, (own, DH), 0)
+            row = (seq * (2 * chips) + place) * own + row
+            angles = row.astype(jnp.float32) * frequency_ref[...]
+            sine = jnp.sin(angles)
+            low = lax.broadcasted_iota(jnp.int32, (own, DH), 1) < DH // 2
+            cos_ref[0, place] = jnp.cos(angles)
+            sin_ref[0, place] = jnp.where(low, -sine, sine)
+            cos_ref[1, place] = jnp.ones((own, DH), jnp.float32)
+            sin_ref[1, place] = jnp.zeros((own, DH), jnp.float32)
+        lane = lax.broadcasted_iota(jnp.int32, tables.shape, 1)
+        choice = jnp.zeros(tables.shape, jnp.int32)
+        for head in range(H):
+            choice = jnp.where(lane == head, choice_ref[head], choice)
+        slot = GROUP * choice
+        for head in range(H):
+            slot = slot + jnp.where((choice == choice_ref[head]) & (lane > head), 1, 0)
+        tables[...] = slot
+        copy = pltpu.make_async_copy(tables, slot_ref, table_sem)
+        copy.start()
+        copy.wait()
+        order = jnp.zeros(tables.shape, jnp.int32)
+        for head in range(H):
+            order = order + jnp.where(lane == slot_ref[0, head], head, 0)
+        tables[...] = order
+        copy = pltpu.make_async_copy(tables, index_ref, table_sem)
+        copy.start()
+        copy.wait()
 
     def give(where, k, c, target):
         send(
@@ -143,47 +172,79 @@
         copy.start()
         locals_.append(copy)
 
-    def project(c):
+    def relay(c):
         for other in others:
             block = x_all.at[other, core, rows_of(c)]
             arrived(block, x_sem.at[other, core, c], "tp", other * 2 + core)
             send(block, block, x_sem.at[other, core, c], "tp", partner)
-        for other in others:
+
+    def project(c):
+        for where in [chip] + others:
             arrived(
-                x_all.at[other, 1 - core, rows_of(c)], x_sem.at[other, 1 - core, c], "tp", partner
-            )
-            compute(other, c * part, part, False)
+                x_all.at[where, 1 - core, rows_of(c)], x_sem.at[where, 1 - core, c], "tp", partner
+            )
+        compute(c)
+        for other in others:
             for k in range(2):
                 give(other, k, c, other * 2 + k)
+        keeps[c].start()
+        give(chip, 1 - core, c, partner)
         if c + ahead < parts:
             send_tokens(c + ahead)
 
+    def home(j):
+        return j * here // GROUP // kv_per // 2
+
+    def fill(where, c):
+        @pl.loop(0, seq_count // chips)
+        def _(k):
+            j = where * (seq_count // chips) + k
+            kv_head = j * here // GROUP
+            for n in range(2):
+                sent[j, here + n, rows_of(c)] = landed[c][
+                    kv_head // kv_per, q_per + n * kv_per + kv_head % kv_per
+                ]
+
+    def kv_send(c, k):
+        j = near[k]
+        return j, pltpu.make_async_remote_copy(
+            src_ref=sent.at[j, pl.ds(here, 2), rows_of(c)],
+            dst_ref=kv_ref.at[tp, seq, :, rows_of(c)],
+            send_sem=kv_send_sem.at[c, k], recv_sem=kv_sem.at[seq, c],
+            device_id={"seq": j}, device_id_type=MESH,
+        )
+
+    kv_sends = [[kv_send(c, k) for k in range(seq_count - 1)] for c in range(parts)]
+
+    def early(c):
+        keeps[c].wait()
+        arrived(landed[c].at[partner], land_sem.at[partner, c], "tp", partner)
+        fill(chip, c)
+        for j, copy in kv_sends[c]:
+
+            @pl.when(home(j) == chip)
+            def _():
+                copy.start()
+
     def exchange(c):
         rows = rows_of(c)
-        keeps[c].wait()
-        for k in range(1, tp_count):
-            source = (tp + k) % tp_count
-            arrived(landed[c].at[source], land_sem.at[source, c], "tp", source)
-
-        @pl.loop(0, seq_count)
-        def _(j):
-            kv_head = j * here // GROUP
+        for other in others:
             for k in range(2):
-                sent[j, here + k, rows] = landed[c][
-                    kv_head // kv_per, q_per + k * kv_per + kv_head % kv_per
-                ]
-
-        for j in near:
-            send(
-                sent.at[j, pl.ds(here, 2), rows], kv_ref.at[tp, seq, :, rows],
-                kv_sem.at[seq, c], "seq", j,
-            )
+                source = other * 2 + k
+                arrived(landed[c].at[source], land_sem.at[source, c], "tp", source)
+            fill(other, c)
+        for j, copy in kv_sends[c]:
+
+            @pl.when(home(j) != chip)
+            def _():
+                copy.start()
+
         hold(sent.at[seq, pl.ds(here, 2), rows], kv_ref.at[tp, seq, :, rows], hold_sem.at[0, c])
 
         @pl.loop(0, seq_count)
         def _(j):
             for k in range(here):
-                head = index_ref[j * here + k]
+                head = index_ref[0, j * here + k]
                 sent[j, k, rows] = landed[c][head // q_per, head % q_per]
 
         for j in near:
@@ -210,25 +271,25 @@
             arrived(block, spread_sem.at[far, c], "tp", far)
             send(block, block, spread_sem.at[far, c], "tp", partner)
 
-    own_copy.wait()
-    for c in range(parts):
-        arrived(x_all.at[chip, 1 - core, rows_of(c)], x_sem.at[chip, 1 - core, c], "tp", partner)
-    compute(chip, 0, own, True)
+    make_tables()
     keeps = [
         pltpu.make_async_copy(
             stage.at[chip, core, :, rows_of(c)], landed[c].at[tp], keep_sem.at[c]
         )
         for c in range(parts)
     ]
-    for c in range(parts):
-        keeps[c].start()
-        give(chip, 1 - core, c, partner)
-
+    own_copy.wait()
+    relay(0)
     for step in range(parts + 3):
         if step < parts:
             project(step)
+            if step == 0 and parts > 1:
+                relay(1)
+            early(step)
         if 0 <= step - 1 < parts:
             exchange(step - 1)
+        if 1 < step + 1 < parts:
+            relay(step + 1)
         if 0 <= step - 2 < parts:
             spread(step - 2)
         if 0 <= step - 3 < parts:
@@ -326,28 +387,31 @@
         ).wait_recv()
 
     for head in range(seq_count * here):
-        slot = slot_ref[head]
+        slot = slot_ref[0, head]
         out_ref[:, head * DH : (head + 1) * DH] = final[slot // here, slot % here]
 
     @pl.loop(1, seq_count)
     def _(change):
         outgoing(change)[1].wait_send()
+    for copies in kv_sends:
+        for _, copy in copies:
+            copy.wait_send()
     for copy in sends:
         copy.wait_send()
 
 
 PARTS = 4
 AHEAD = 2
+STEP_HEADS = 4
 
 
 def layer(
-    index, slot, document_index, tokens, w, down, up, cosine, sine, tp_count, seq_count,
-    rotated_heads,
+    choice, document_index, tokens, w, down, up, frequency, tp_count, seq_count, rotated
 ):
     own, width = tokens.shape
     heads = w.shape[1] // DH
-    pair = 2
-    steps = heads // pair
+    group = STEP_HEADS
+    steps = heads // group
     chips = tp_count // 2
     here = H // seq_count
     rank = down.shape[1]
@@ -355,25 +419,30 @@
     vmem = pl.BlockSpec(memory_space=pltpu.VMEM)
     smem = pl.BlockSpec(memory_space=pltpu.SMEM)
     anywhere = pl.BlockSpec(memory_space=pl.ANY)
-    count = 3 * parts * (2 * (chips - 1) + 1) + 2 * parts * (seq_count - 1)
-    bf16 = jnp.bfloat16
+    count = 3 * parts * (2 * (chips - 1) + 1) + parts * (seq_count - 1)
+    bf16, f32 = jnp.bfloat16, jnp.float32
     dma = pltpu.SemaphoreType.DMA
     mine = (seq_count, here, own, DH)
     return pl.pallas_call(
-        functools.partial(layer_kernel, rotated_heads // pair, here, AHEAD),
-        in_specs=[smem, smem, vmem, anywhere, anywhere, vmem, vmem, vmem, vmem],
+        functools.partial(layer_kernel, rotated, here, AHEAD),
+        in_specs=[smem, vmem, vmem, anywhere, anywhere, vmem, vmem],
         out_specs=vmem,
         out_shape=jax.ShapeDtypeStruct((own, H * DH), bf16),
         scratch_shapes=[
             pltpu.VMEM((chips, 2, own, width), bf16),
-            pltpu.VMEM((steps, width, pair * DH), bf16),
+            pltpu.VMEM((steps, width, group * DH), bf16),
             pltpu.VMEM((chips, 2, heads, own, DH), bf16),
             pltpu.VMEM((seq_count, here + 2, own, DH), bf16),
-            pltpu.VMEM((2 * own, rank), bf16),
+            pltpu.VMEM((tp_count * own // parts, rank), bf16),
             pltpu.VMEM(mine, bf16),
             pltpu.VMEM((tp_count, seq_count, 2, own, DH), bf16),
             pltpu.VMEM(mine, bf16),
             pltpu.VMEM(mine, bf16),
+            pltpu.VMEM((2, tp_count, own, DH), f32),
+            pltpu.VMEM((2, tp_count, own, DH), f32),
+            pltpu.VMEM((8, 128), jnp.int32),
+            pltpu.SMEM((8, 128), jnp.int32),
+            pltpu.SMEM((8, 128), jnp.int32),
             dma((steps,)),
             dma(()),
             dma((parts,)),
@@ -386,22 +455,13 @@
             dma((tp_count, parts)),
             dma((seq_count,)),
             dma((seq_count,)),
+            dma((parts, seq_count - 1)),
+            dma(()),
         ]
         + [pltpu.VMEM((tp_count, heads, own // parts, DH), bf16)] * parts,
         compiler_params=pltpu.CompilerParams(collective_id=0, has_side_effects=True),
         name="layer",
-    )(
-        index, slot, document_index.reshape(-1, own), tokens, w, down.T, up, cosine, sine,
-    )
-
-
-def head_tables(query_to_key_head):
-    heads = jnp.arange(H, dtype=jnp.int32)
-    same = query_to_key_head[:, None] == query_to_key_head[None, :]
-    earlier = heads[None, :] < heads[:, None]
-    slot = GROUP * query_to_key_head + jnp.sum((same & earlier).astype(jnp.int32), 1)
-    order = jnp.sum(jnp.where(slot[None, :] == heads[:, None], heads[None, :], 0), 1)
-    return order.astype(jnp.int32), slot.astype(jnp.int32)
+    )(choice, document_index.reshape(-1, own), frequency, tokens, w, down.T, up)
 
 
 def per_device(
@@ -414,22 +474,11 @@
 ):
     tp_count = lax.axis_size("tp")
     seq_count = lax.axis_size("seq")
-    tp_rank = lax.axis_index("tp")
-    seq_rank = lax.axis_index("seq")
-    own = tokens.shape[0]
-    block = own * tp_count
-    here = H // seq_count
-    q_per, kv_per = H // tp_count, KV // tp_count
-
-    index, slot = head_tables(query_to_key_head)
-    places = (seq_rank * block + jnp.arange(block, dtype=jnp.int32)).astype(jnp.float32)
-    cosine, sine = rope_tables(places)
-    table = (1, tp_count // 2, 2, own, DH)
-    cosine = jnp.concatenate([cosine.reshape(table), jnp.ones(table, jnp.float32)])
-    sine = jnp.concatenate([sine.reshape(table), jnp.zeros(table, jnp.float32)])
+    frequency = THETA ** (-(jnp.arange(DH // 2, dtype=jnp.float32) * 2.0) / DH)
+    frequency = jnp.concatenate([frequency, frequency])[None, :]
     return layer(
-        index, slot, document_index, tokens, joined_projection_weight, adapter_down_weight,
-        adapter_up_weight, cosine, sine, tp_count, seq_count, q_per + kv_per,
+        query_to_key_head, document_index, tokens, joined_projection_weight, adapter_down_weight,
+        adapter_up_weight, frequency, tp_count, seq_count, (H + KV) // tp_count,
     )
 
 

time: 108 us -> 104 us (0.963)
  the two profiles are of different devices: /device:TPU:13 before, /device:TPU:0 now
where the time goes in v4:
time: 104 us
  Pallas kernels  101 us (97%)
  local copies, waits for them, and re-layouts  2.29 us (2%)
    pallas_call x1, Pallas kernels, layer(): pl.pallas_call(functools.partial(layer_kernel, rotated, here, AHEAD), in_...  101 us
    unnamed x1, local copies, waits for them, and re-layouts  2.29 us

profile of v4, /device:TPU:0, one launch (start us, length us, event | category | flops | bytes accessed | tf_op | source)
XLA Modules:
  0.0 103.5 jit_solution(11021829706676609257)
XLA Ops:
  0.0 0.6 maximum_bitcast_fusion.frequency_ref
  0.6 100.6 %layer.1 = bf16[128,4096]{1,0:T(8,128)(2,1)} custom-call(s32[32]{0:T(128)} %choice_ref.1, s32[32,128]{1,0:T(8,128)} %bitcast.5, f32[1,128]{1,0:T(1,128)} %maximum_bitcast_fusion.frequency_ref, bf16[128,4096]{1,0:T(8,128)(2,1)} %tokens_ref.1, bf16[4096,1536]{1,0:T(8,128)(2,1)} %w_ref.1, bf16[64,4096]{1,0:T(8,128)(2,1)} %bitcast.4, bf16[64,1536]{1,0:T(8,128)(2,1)} %up_ref.1), custom_call_target="tpu_custom_call" | custom-call | tf_op jit(solution)/shard_map/layer/pallas_call | solution.py:426
  101.3 2.3 %copy.8 = bf16[128,4096]{1,0:T(8,128)(2,1)} copy(bf16[128,4096]{1,0:T(8,128)(2,1)} %layer.1) | data formatting | bytes 2097152
  (1 shorter events, 0.0 us)

commit v5 on v4

--- a/solution.py
+++ b/solution.py
@@ -26,6 +26,7 @@
     out_ref,
     x_all, w_all, stage, sent, mid_ref, q_ref, kv_ref, context, final, cos_ref, sin_ref,
     tables, slot_ref, index_ref,
+    landed_kv,
     w_sem, own_sem, keep_sem, hold_sem, send_sem, x_sem, land_sem, q_sem, kv_sem, spread_sem,
     give_sem, final_sem, kv_send_sem, table_sem, *landed,
 ):
@@ -44,7 +45,7 @@
     q_per = H // tp_count
     kv_per = KV // tp_count
     sends = []
-    locals_ = []
+    q_steps = q_per // group
 
     def send(src, dst, sem, axis, target):
         copy = pltpu.make_async_remote_copy(
@@ -70,7 +71,7 @@
 
     own_copy = pltpu.make_async_copy(tokens_ref, x_all.at[chip, core], own_sem)
     own_copy.start()
-    for step in range(steps):
+    for step in list(range(q_steps, steps)) + list(range(q_steps)):
         weight_copy(step).start()
 
     barrier = pltpu.get_barrier_semaphore()
@@ -99,15 +100,11 @@
             x_sem.at[chip, core, c], "tp", partner,
         )
 
-    def compute(c):
+    def compute(c, first, last):
         rows = rows_of(c)
         count = 2 * chips * part
-        mid_ref[...] = lax.dot_general(
-            x_all[:, :, rows, :].reshape(count, width), down_ref[...], (((1,), (1,)), ((), ())),
-            preferred_element_type=jnp.float32,
-        ).astype(jnp.bfloat16)
-
-        @pl.loop(0, steps)
+
+        @pl.loop(first, last)
         def _(step):
             if c == 0:
                 weight_copy(step).wait()
@@ -116,7 +113,7 @@
                 preferred_element_type=jnp.float32,
             )
             joined = joined + ADAPTER_SCALE * jnp.dot(
-                mid_ref[...], up_ref[:, pl.ds(pl.multiple_of(step * wide, wide), wide)],
+                mid_ref[c], up_ref[:, pl.ds(pl.multiple_of(step * wide, wide), wide)],
                 preferred_element_type=jnp.float32
             )
             for n in range(group):
@@ -162,15 +159,27 @@
         copy.start()
         copy.wait()
 
-    def give(where, k, c, target):
+    kv_heads, q_heads = pl.ds(q_per, 2 * kv_per), pl.ds(0, q_per)
+
+    def keep(kind, c):
+        heads, dst = ((kv_heads, landed_kv.at[c, tp]), (q_heads, landed[c].at[tp]))[kind]
+        return pltpu.make_async_copy(
+            stage.at[chip, core, heads, rows_of(c)], dst, keep_sem.at[kind, c]
+        )
+
+    def give(kind, c):
+        heads, dst = ((kv_heads, landed_kv.at[c, tp]), (q_heads, landed[c].at[tp]))[kind]
+        for other in others:
+            for k in range(2):
+                send(
+                    stage.at[other, k, heads, rows_of(c)], dst, land_sem.at[kind, tp, c], "tp",
+                    other * 2 + k,
+                )
+        keep(kind, c).start()
         send(
-            stage.at[where, k, :, rows_of(c)], landed[c].at[tp], land_sem.at[tp, c], "tp", target
-        )
-
-    def hold(src, dst, sem):
-        copy = pltpu.make_async_copy(src, dst, sem)
-        copy.start()
-        locals_.append(copy)
+            stage.at[chip, 1 - core, heads, rows_of(c)], dst, land_sem.at[kind, tp, c], "tp",
+            partner,
+        )
 
     def relay(c):
         for other in others:
@@ -178,19 +187,23 @@
             arrived(block, x_sem.at[other, core, c], "tp", other * 2 + core)
             send(block, block, x_sem.at[other, core, c], "tp", partner)
 
-    def project(c):
+    def project_kv(c):
         for where in [chip] + others:
             arrived(
                 x_all.at[where, 1 - core, rows_of(c)], x_sem.at[where, 1 - core, c], "tp", partner
             )
-        compute(c)
-        for other in others:
-            for k in range(2):
-                give(other, k, c, other * 2 + k)
-        keeps[c].start()
-        give(chip, 1 - core, c, partner)
+        mid_ref[c] = lax.dot_general(
+            x_all[:, :, rows_of(c), :].reshape(2 * chips * part, width), down_ref[...],
+            (((1,), (1,)), ((), ())), preferred_element_type=jnp.float32,
+        ).astype(jnp.bfloat16)
+        compute(c, q_steps, steps)
+        give(0, c)
         if c + ahead < parts:
             send_tokens(c + ahead)
+
+    def project_q(c):
+        compute(c, 0, q_steps)
+        give(1, c)
 
     def home(j):
         return j * here // GROUP // kv_per // 2
@@ -201,8 +214,8 @@
             j = where * (seq_count // chips) + k
             kv_head = j * here // GROUP
             for n in range(2):
-                sent[j, here + n, rows_of(c)] = landed[c][
-                    kv_head // kv_per, q_per + n * kv_per + kv_head % kv_per
+                sent[j, here + n, rows_of(c)] = landed_kv[
+                    c, kv_head // kv_per, n * kv_per + kv_head % kv_per
                 ]
 
     def kv_send(c, k):
@@ -217,8 +230,8 @@
     kv_sends = [[kv_send(c, k) for k in range(seq_count - 1)] for c in range(parts)]
 
     def early(c):
-        keeps[c].wait()
-        arrived(landed[c].at[partner], land_sem.at[partner, c], "tp", partner)
+        keep(0, c).wait()
+        arrived(landed_kv.at[c, partner], land_sem.at[0, partner, c], "tp", partner)
         fill(chip, c)
         for j, copy in kv_sends[c]:
 
@@ -226,12 +239,11 @@
             def _():
                 copy.start()
 
-    def exchange(c):
-        rows = rows_of(c)
+    def exchange_kv(c):
         for other in others:
             for k in range(2):
                 source = other * 2 + k
-                arrived(landed[c].at[source], land_sem.at[source, c], "tp", source)
+                arrived(landed_kv.at[c, source], land_sem.at[0, source, c], "tp", source)
             fill(other, c)
         for j, copy in kv_sends[c]:
 
@@ -239,7 +251,26 @@
             def _():
                 copy.start()
 
-        hold(sent.at[seq, pl.ds(here, 2), rows], kv_ref.at[tp, seq, :, rows], hold_sem.at[0, c])
+        hold_kv(c).start()
+
+    def hold_kv(c):
+        rows = rows_of(c)
+        return pltpu.make_async_copy(
+            sent.at[seq, pl.ds(here, 2), rows], kv_ref.at[tp, seq, :, rows], hold_sem.at[0, c]
+        )
+
+    def hold_q(c):
+        rows = rows_of(c)
+        return pltpu.make_async_copy(
+            sent.at[seq, pl.ds(0, here), rows], q_ref.at[seq, :, rows], hold_sem.at[1, c]
+        )
+
+    def exchange_q(c):
+        rows = rows_of(c)
+        keep(1, c).wait()
+        for k in range(1, tp_count):
+            source = (tp + k) % tp_count
+            arrived(landed[c].at[source], land_sem.at[1, source, c], "tp", source)
 
         @pl.loop(0, seq_count)
         def _(j):
@@ -252,11 +283,11 @@
                 sent.at[j, pl.ds(0, here), rows], q_ref.at[seq, :, rows],
                 q_sem.at[seq, c], "seq", j,
             )
-        hold(sent.at[seq, pl.ds(0, here), rows], q_ref.at[seq, :, rows], hold_sem.at[1, c])
+        hold_q(c).start()
 
     def spread(c):
         rows = rows_of(c)
-        locals_[2 * c].wait()
+        hold_kv(c).wait()
         for source in near:
             arrived(kv_ref.at[tp, source, :, rows], kv_sem.at[source, c], "seq", source)
         block = kv_ref.at[tp, :, :, rows]
@@ -272,37 +303,35 @@
             send(block, block, spread_sem.at[far, c], "tp", partner)
 
     make_tables()
-    keeps = [
-        pltpu.make_async_copy(
-            stage.at[chip, core, :, rows_of(c)], landed[c].at[tp], keep_sem.at[c]
-        )
-        for c in range(parts)
-    ]
     own_copy.wait()
     relay(0)
-    for step in range(parts + 3):
-        if step < parts:
-            project(step)
-            if step == 0 and parts > 1:
+    for c in range(parts + 4):
+        if c < parts:
+            project_kv(c)
+            if c == 0 and parts > 1:
                 relay(1)
-            early(step)
-        if 0 <= step - 1 < parts:
-            exchange(step - 1)
-        if 1 < step + 1 < parts:
-            relay(step + 1)
-        if 0 <= step - 2 < parts:
-            spread(step - 2)
-        if 0 <= step - 3 < parts:
-            forward(step - 3)
+            early(c)
+        if 0 <= c - 1 < parts:
+            exchange_kv(c - 1)
+        if 0 <= c - 2 < parts:
+            project_q(c - 2)
+        if 0 <= c - 3 < parts:
+            spread(c - 3)
+            exchange_q(c - 3)
+        if 0 <= c - 4 < parts:
+            forward(c - 4)
+        if 1 < c + 1 < parts:
+            relay(c + 1)
 
     for c in range(parts):
-        locals_[2 * c + 1].wait()
+        hold_q(c).wait()
         for k in range(chips):
             source = (chip + k) % chips * 2 + 1 - core
             arrived(kv_ref.at[source, :, :, rows_of(c)], spread_sem.at[source, c], "tp", partner)
 
     block = tp_count * own
-    rows = here * own
+    slab = own // BANDS
+    rows = here * slab
     factor = (DH**-0.5) * LOG2_E
 
     def toggled(change):
@@ -313,12 +342,15 @@
             bit *= 2
         return result
 
-    def attend(step):
-        q = q_ref[step].reshape(rows, DH)
+    def band_of(band):
+        return pl.ds(band * slab, slab)
+
+    def attend(step, band):
+        q = q_ref[step, :, band_of(band)].reshape(rows, DH)
         docs = doc_ref[pl.ds(step * tp_count + tp, 1), :]
-        docs = jnp.broadcast_to(docs, (own, own)).T[:, :1]
+        docs = jnp.broadcast_to(docs, (own, own)).T[band * slab : (band + 1) * slab, :1]
         docs = jnp.concatenate([docs] * here, 0)
-        places = tp * own + lax.broadcasted_iota(jnp.int32, (own, 1), 0)
+        places = tp * own + band * slab + lax.broadcasted_iota(jnp.int32, (slab, 1), 0)
         places = jnp.concatenate([places] * here, 0)
 
         def body(index, carry, own_block=False):
@@ -350,41 +382,46 @@
             jnp.zeros((rows, DH), jnp.float32),
         )
         _, total, acc = lax.fori_loop(0, step, body, body(step, start, True))
-        return (acc / total).astype(jnp.bfloat16).reshape(here, own, DH)
-
-    def outgoing(change):
+        return (acc / total).astype(jnp.bfloat16).reshape(here, slab, DH)
+
+    def outgoing(change, band):
         target = toggled(change)
         return target, pltpu.make_async_remote_copy(
-            src_ref=context.at[change], dst_ref=final.at[seq], send_sem=give_sem.at[change],
-            recv_sem=final_sem.at[seq], device_id={"seq": target}, device_id_type=MESH,
-        )
-
-    def hand(change):
-        target, copy = outgoing(change)
-        for c in range(parts):
+            src_ref=context.at[change, :, band_of(band)], dst_ref=final.at[seq, :, band_of(band)],
+            send_sem=give_sem.at[change, band], recv_sem=final_sem.at[seq, band],
+            device_id={"seq": target}, device_id_type=MESH,
+        )
+
+    def hand(change, band):
+        target, copy = outgoing(change, band)
+        for c in range(band * parts // BANDS, (band + 1) * parts // BANDS):
             arrived(q_ref.at[target, :, rows_of(c)], q_sem.at[target, c], "seq", target)
-        context[change] = attend(target)
+        context[change, :, band_of(band)] = attend(target, band)
         copy.start()
 
     half = seq_count // 2
-
-    @pl.loop(0, half)
-    def _(i):
-        hand(half + i)
-
-    @pl.loop(0, half - 1)
-    def _(i):
-        hand(half - 1 - i)
-
-    final[seq] = attend(seq)
+    for band in range(BANDS):
+
+        @pl.loop(0, half)
+        def _(i):
+            hand(half + i, band)
+
+        @pl.loop(0, half - 1)
+        def _(i):
+            hand(half - 1 - i, band)
+
+        final[seq, :, band_of(band)] = attend(seq, band)
 
     @pl.loop(1, seq_count)
     def _(change):
         source = toggled(change)
-        pltpu.make_async_remote_copy(
-            src_ref=final.at[source], dst_ref=final.at[source], send_sem=give_sem.at[0],
-            recv_sem=final_sem.at[source], device_id={"seq": source}, device_id_type=MESH,
-        ).wait_recv()
+        for band in range(BANDS):
+            dst = final.at[source, :, band_of(band)]
+            pltpu.make_async_remote_copy(
+                src_ref=dst, dst_ref=dst, send_sem=give_sem.at[0, 0],
+                recv_sem=final_sem.at[source, band], device_id={"seq": source},
+                device_id_type=MESH,
+            ).wait_recv()
 
     for head in range(seq_count * here):
         slot = slot_ref[0, head]
@@ -392,7 +429,8 @@
 
     @pl.loop(1, seq_count)
     def _(change):
-        outgoing(change)[1].wait_send()
+        for band in range(BANDS):
+            outgoing(change, band)[1].wait_send()
     for copies in kv_sends:
         for _, copy in copies:
             copy.wait_send()
@@ -403,6 +441,7 @@
 PARTS = 4
 AHEAD = 2
 STEP_HEADS = 4
+BANDS = 1
 
 
 def layer(
@@ -419,7 +458,8 @@
     vmem = pl.BlockSpec(memory_space=pltpu.VMEM)
     smem = pl.BlockSpec(memory_space=pltpu.SMEM)
     anywhere = pl.BlockSpec(memory_space=pl.ANY)
-    count = 3 * parts * (2 * (chips - 1) + 1) + parts * (seq_count - 1)
+    q_per = H // tp_count
+    count = 4 * parts * (2 * (chips - 1) + 1) + parts * (seq_count - 1)
     bf16, f32 = jnp.bfloat16, jnp.float32
     dma = pltpu.SemaphoreType.DMA
     mine = (seq_count, here, own, DH)
@@ -433,7 +473,7 @@
             pltpu.VMEM((steps, width, group * DH), bf16),
             pltpu.VMEM((chips, 2, heads, own, DH), bf16),
             pltpu.VMEM((seq_count, here + 2, own, DH), bf16),
-            pltpu.VMEM((tp_count * own // parts, rank), bf16),
+            pltpu.VMEM((parts, tp_count * own // parts, rank), bf16),
             pltpu.VMEM(mine, bf16),
             pltpu.VMEM((tp_count, seq_count, 2, own, DH), bf16),
             pltpu.VMEM(mine, bf16),
@@ -443,22 +483,23 @@
             pltpu.VMEM((8, 128), jnp.int32),
             pltpu.SMEM((8, 128), jnp.int32),
             pltpu.SMEM((8, 128), jnp.int32),
+            pltpu.VMEM((parts, tp_count, heads - q_per, own // parts, DH), bf16),
             dma((steps,)),
             dma(()),
-            dma((parts,)),
+            dma((2, parts)),
             dma((2, parts)),
             dma((count,)),
             dma((chips, 2, parts)),
-            dma((tp_count, parts)),
+            dma((2, tp_count, parts)),
             dma((seq_count, parts)),
             dma((seq_count, parts)),
             dma((tp_count, parts)),
-            dma((seq_count,)),
-            dma((seq_count,)),
+            dma((seq_count, BANDS)),
+            dma((seq_count, BANDS)),
             dma((parts, seq_count - 1)),
             dma(()),
         ]
-        + [pltpu.VMEM((tp_count, heads, own // parts, DH), bf16)] * parts,
+        + [pltpu.VMEM((tp_count, q_per, own // parts, DH), bf16)] * parts,
         compiler_params=pltpu.CompilerParams(collective_id=0, has_side_effects=True),
         name="layer",
     )(choice, document_index.reshape(-1, own), frequency, tokens, w, down.T, up)

time: 104 us -> 100 us (0.962)
  the two profiles are of different devices: /device:TPU:0 before, /device:TPU:13 now
where the time goes in v5:
time: 100 us
  Pallas kernels  97.3 us (97%)
  local copies, waits for them, and re-layouts  2.29 us (2%)
    pallas_call x1, Pallas kernels, layer(): pl.pallas_call(functools.partial(layer_kernel, rotated, here, AHEAD), in_...  97.3 us
    unnamed x1, local copies, waits for them, and re-layouts  2.29 us

profile of v5, /device:TPU:13, one launch (start us, length us, event | category | flops | bytes accessed | tf_op | source)
XLA Modules:
  0.0 100.2 jit_solution(11715106505511331698)
XLA Ops:
  0.0 0.6 maximum_bitcast_fusion.frequency_ref
  0.6 97.3 %layer.1 = bf16[128,4096]{1,0:T(8,128)(2,1)} custom-call(s32[32]{0:T(128)} %choice_ref.1, s32[32,128]{1,0:T(8,128)} %bitcast.5, f32[1,128]{1,0:T(1,128)} %maximum_bitcast_fusion.frequency_ref, bf16[128,4096]{1,0:T(8,128)(2,1)} %tokens_ref.1, bf16[4096,1536]{1,0:T(8,128)(2,1)} %w_ref.1, bf16[64,4096]{1,0:T(8,128)(2,1)} %bitcast.4, bf16[64,1536]{1,0:T(8,128)(2,1)} %up_ref.1), custom_call_target="tpu_custom_call" | custom-call | tf_op jit(solution)/shard_map/layer/pallas_call | solution.py:466
  97.9 2.3 %copy.8 = bf16[128,4096]{1,0:T(8,128)(2,1)} copy(bf16[128,4096]{1,0:T(8,128)(2,1)} %layer.1) | data formatting | bytes 2097152
  (1 shorter events, 0.0 us)
